TPU v7x, 128 devices: a whole 4x4x4 slice. The times are simulated.
128 devices in a mesh: gx: 16 (over y, x_hi, core), gy: 8 (over x_lo, z).
Axes of the slice: x: 4 (x_hi: 2, x_lo: 2; x = x_hi * 2 + x_lo), y: 4, z: 4, core: 2. Of those that a mesh axis runs over, the one named last changes fastest.
Arguments:
- mixing: float32 [3, 8, 128, 1024], P(None, None, 'gx', 'gy'), may hold values from 0.02 to 0.5
- forcing: float32 [2, 8, 128, 1024], P(None, None, 'gx', 'gy'), may hold values from -6 to 6
- labels: int32 [8, 128, 1024], P(None, 'gx', 'gy'), may hold values from 0 to 2
- colours: int32 [16, 8], P('gx', 'gy'), may hold values from 0 to 5
- coarse_basis: float32 [2, 8, 128, 1024], P(None, None, 'gx', 'gy'), may hold values from 0.5 to 2
- coarse_inverse: float32 [16, 8, 2, 256], P('gx', 'gy'), may hold values from -4 to 4
Outputs:
- concentration: float32 [2, 8, 128, 1024], P(None, None, 'gx', 'gy')
- coarse_coeff: float32 [16, 8, 2], P('gx', 'gy')
All inputs are finite; a program needn't handle non-finite values.
Results may differ from a plain program's by a relative error of at most 0.0003.
Values sent between devices are 32-bit elements; how exact they have to be, the bound alone decides.
No kernel may reach another device: no remote copies, remote signals or barrier semaphores. Data moves between devices by JAX's collectives and lax.ppermute only.
A program may use at most 64 MiB of HBM per device.

v0:
```python
import jax
import jax.numpy as jnp
from jax import lax
from jax.experimental import pallas as pl
from jax.experimental.pallas import tpu as pltpu
from jax.sharding import PartitionSpec as P

SWEEPS = 20
OMEGA = 0.8
UNROLL = 19
PAD = 8
WIN = (16, 13, 10, 7, 4)
KEEP = (104, 80, 56, 32, 8)
ROWS = 400
F32 = jnp.float32
NGX = 16
NGY = 8


def iota(shape, dim):
    return lax.broadcasted_iota(jnp.int32, shape, dim)


def roll(x, by, axis):
    by = by % x.shape[axis]
    return x if by == 0 else pltpu.roll(x, by, axis)


def lane_ids():
    lane = iota((8, 128), 1)
    return lane & 15, lane >> 4


def edge_columns(tiles):
    lane = iota((8, 128), 1)
    out = jnp.zeros((8, 128), F32)
    for n, tile in enumerate(tiles):
        out = jnp.where(lane == n, roll(tile, n, 1), out)
        out = jnp.where(lane == 16 + n, roll(tile, 17 + n, 1), out)
    return out


def pack_kernel(mix, forc, lab, basis, colour, out, lab_v, basis_v, sems):
    copies = [
        pltpu.make_async_copy(basis, basis_v, sems.at[0]),
        pltpu.make_async_copy(lab, lab_v, sems.at[1]),
    ]
    for f in range(3):
        copies.append(pltpu.make_async_copy(mix.at[f], out.at[pl.ds(f * 8, 8)], sems.at[3 + f]))
    for f in range(2):
        copies.append(pltpu.make_async_copy(forc.at[f], out.at[pl.ds(24 + f * 8, 8)], sems.at[6 + f]))
    for c in copies:
        c.start()
    for c in copies:
        c.wait()
    out[40:48] = lab_v[...].astype(F32)
    cols = edge_columns([basis_v[f, z] for f in range(2) for z in range(8)])
    lane = iota((8, 128), 1)
    out[48] = jnp.where(lane == 32, colour[...].astype(F32), cols)


def rows_kernel(own, left, right, basis, first, second):
    even = lax.axis_index("gx") % 2 == 0
    pl.when(even)(lambda: write_rows(own, left, right, basis, second, first))
    pl.when(jnp.logical_not(even))(lambda: write_rows(own, left, right, basis, first, second))


def write_rows(own, left, right, basis, up, down):
    for part, ref in enumerate((left, own, right)):
        lanes = slice(part * 128, part * 128 + 128)
        for a in range(6):
            for p in range(4):
                lo, hi = ref[a * 8 + 2 * p], ref[a * 8 + 2 * p + 1]
                sub = iota((8, 128), 0)
                up[a * 4 + p, :, lanes] = jnp.where(sub < 4, lo, roll(hi, 4, 0))
                down[a * 4 + p, :, lanes] = jnp.where(sub < 4, roll(lo, 4, 0), hi)
        for z in range(8):
            up[24, z : z + 1, lanes] = ref[40 + z, 4:5, :]
            down[24, z : z + 1, lanes] = ref[40 + z, 3:4, :]
            for f in range(2):
                if part == 1:
                    up[25 + f, z : z + 1, lanes] = basis[f, z, 0:1, :]
                    down[25 + f, z : z + 1, lanes] = basis[f, z, 7:8, :]
        if part != 1:
            up[25:27, :, lanes] = jnp.zeros((2, 8, 128), F32)
            down[25:27, :, lanes] = jnp.zeros((2, 8, 128), F32)


def window_rows(kind, tiles):
    if kind == 0:
        return PAD + 128 - 4
    if kind == 1:
        return PAD + 128 + 4 - 8 * tiles
    return PAD + 128 + 124


def prepare(kind, tiles, stat, u, uo, coef, i, j):
    row0 = window_rows(kind, tiles)
    xp, z = lane_ids()
    sub = iota((8, 128), 0)
    rim_x = ((xp == 0) | (xp == 15)).astype(F32)
    gx = i * 8 + xp - 4
    in_x = ((gx >= 0) & (gx < NGX * 8)).astype(F32)
    for t in range(tiles):
        at = pl.ds(row0 + t, 8, stride=tiles)
        s11, s22, s12 = stat[0, at, :], stat[1, at, :], stat[2, at, :]
        y = row0 - PAD - 128 + sub * tiles + t + j * 128
        inside = in_x * ((y >= 0) & (y < NGY * 128)).astype(F32)
        diag = 6.0 + rim_x
        if t == 0 and kind != 1:
            diag = diag + (sub == 0).astype(F32)
        if t == tiles - 1 and kind != 2:
            diag = diag + (sub == 7).astype(F32)
        vals = []
        for f in range(2):
            c = u[f, at, :]
            near = u[f, pl.ds(row0 + t - 1, 8, stride=tiles), :] + u[f, pl.ds(row0 + t + 1, 8, stride=tiles), :]
            out = uo[f, at, :]
            near = near + jnp.where(xp == 0, out, roll(c, 1, 1)) + jnp.where(xp == 15, out, roll(c, -1, 1))
            near = near + jnp.where(z == 0, 0.0, roll(c, 16, 1)) + jnp.where(z == 7, 0.0, roll(c, -16, 1))
            vals.append((c, near))
        for f, s in ((0, s11), (1, s22)):
            c, near = vals[f]
            r = stat[3 + f, at, :] - ((s + 6.0) * c + s12 * vals[1 - f][0] - near)
            w = OMEGA * inside / (s + diag)
            coef[f, t] = w
            coef[2 + f, t] = w * s12
            coef[4 + f, t] = w * r


def adjacency():
    a, b = iota((128, 128), 0), iota((128, 128), 1)
    ax, az, bx, bz = a & 15, a >> 4, b & 15, b >> 4
    near_x = (az == bz) & ((ax - bx == 1) | (bx - ax == 1))
    near_z = (ax == bx) & ((az - bz == 1) | (bz - az == 1))
    one = (near_x | near_z).astype(F32).astype(jnp.bfloat16)
    return jnp.concatenate([one, one], 0)


def sweep(e, tiles, coef, adj):
    sub = iota((8, 128), 0)
    flat = jnp.concatenate(e[0] + e[1], 0)
    hi = flat.astype(jnp.bfloat16)
    lo = (flat - hi.astype(F32)).astype(jnp.bfloat16)
    side = jnp.dot(jnp.concatenate([hi, lo], 1), adj, preferred_element_type=F32)
    new = [[], []]
    for f in range(2):
        for t in range(tiles):
            c = e[f][t]
            before = e[f][t - 1] if t else jnp.where(sub == 0, 0.0, roll(e[f][tiles - 1], 1, 0))
            after = e[f][t + 1] if t + 1 < tiles else jnp.where(sub == 7, 0.0, roll(e[f][0], -1, 0))
            at = (f * tiles + t) * 8
            near = before + after + side[at : at + 8]
            new[f].append((1.0 - OMEGA) * c + coef[4 + f, t] + (coef[f, t] * near - coef[2 + f, t] * e[1 - f][t]))
    return new


def sweeps(kind, tiles, u, coef):
    row0 = window_rows(kind, tiles)
    xp, z = lane_ids()
    sub = iota((8, 128), 0)
    adj = adjacency()

    def body(_, flat):
        e = [list(flat[:tiles]), list(flat[tiles:])]
        for _ in range(UNROLL):
            e = sweep(e, tiles, coef, adj)
        return tuple(e[0] + e[1])

    flat = tuple(coef[4 + f, t] for f in range(2) for t in range(tiles))
    for _ in range((SWEEPS - 1) % UNROLL):
        e = sweep([list(flat[:tiles]), list(flat[tiles:])], tiles, coef, adj)
        flat = tuple(e[0] + e[1])
    if SWEEPS - 1 == UNROLL:
        flat = body(0, flat)
    else:
        flat = lax.fori_loop(0, (SWEEPS - 1) // UNROLL, body, flat)
    own_x = (xp >= 4) & (xp < 12)
    for t in range(tiles):
        at = pl.ds(row0 + t, 8, stride=tiles)
        y = row0 - PAD - 128 + sub * tiles + t
        if kind == 0:
            here = own_x & (y >= 0) & (y < 128)
        elif kind == 1:
            here = own_x & (y < 0)
        else:
            here = own_x & (y >= 128)
        for f in range(2):
            u[f, at, :] = u[f, at, :] + jnp.where(here, flat[f * tiles + t], 0.0)


def solve_round(rnd, stat, u, uo, meta, coefs, i, j):
    own = jnp.max(meta[0:8, :])
    left = jnp.max(meta[8:16, :])
    right = jnp.max(meta[16:24, :])
    jobs = [(0, 17, own, coefs[0])]
    if rnd < 5:
        jobs += [(1, WIN[rnd], left, coefs[1]), (2, WIN[rnd], right, coefs[2])]
    for kind, tiles, colour, coef in jobs:
        pl.when(colour == float(rnd))(lambda kind=kind, tiles=tiles, coef=coef: prepare(kind, tiles, stat, u, uo, coef, i, j))
    for kind, tiles, colour, coef in jobs:
        pl.when(colour == float(rnd))(lambda kind=kind, tiles=tiles, coef=coef: sweeps(kind, tiles, u, coef))


def message_items(rnd):
    tiles = (128 + 2 * KEEP[rnd]) // 8
    items = [(f, PAD + 128 - KEEP[rnd] + 8 * q) for f in range(2) for q in range(tiles)]
    third = len(items) // 3
    return [[items[g * third + m] for g in range(3)] for m in range(third)]


def emit(rnd, u, first, second, even):
    xp, _ = lane_ids()

    def write(up, down):
        for m, trio in enumerate(message_items(rnd)):
            tiles = [u[f, pl.ds(row, 8), :] for f, row in trio]
            at = pl.ds(8 * m, 8)
            for ref, lane0 in ((up, 4), (down, 7)):
                a, b, c = (roll(tile, 5 * g - lane0, 1) for g, tile in enumerate(tiles))
                ref[at, :] = jnp.where(xp < 5, a, jnp.where(xp < 10, b, c))

    pl.when(even)(lambda: write(second, first))
    pl.when(jnp.logical_not(even))(lambda: write(first, second))


def absorb(rnd, u, uo, first, second, i):
    xp, _ = lane_ids()
    has_above = (i > 0).astype(F32)
    has_below = (i < NGX - 1).astype(F32)

    def read(above, below):
        for m, trio in enumerate(message_items(rnd)):
            a = above[pl.ds(8 * m, 8), :] * has_above
            b = below[pl.ds(8 * m, 8), :] * has_below
            for g, (f, row) in enumerate(trio):
                at = pl.ds(row, 8)
                inner = jnp.where(xp >= 12, roll(b, 12 - 5 * g, 1), u[f, at, :])
                u[f, at, :] = jnp.where(xp < 4, roll(a, -5 * g - 1, 1), inner)
                uo[f, at, :] = jnp.where(xp == 0, roll(a, -5 * g, 1), roll(b, 11 - 5 * g, 1))

    even = i % 2 == 0
    pl.when(even)(lambda: read(second, first))
    pl.when(jnp.logical_not(even))(lambda: read(first, second))


def start_kernel(own, left, right, first, second, stat, u, meta, fin, out1, out2, near, buf, uo, c0, c1, c2):
    i = lax.axis_index("gx")
    even = i % 2 == 0

    def place(above, below):
        near[0] = above[...]
        near[1] = below[...]

    pl.when(even)(lambda: place(second, first))
    pl.when(jnp.logical_not(even))(lambda: place(first, second))
    above, below = near.at[0], near.at[1]
    j = lax.axis_index("gy")
    xp, _ = lane_ids()
    lane = iota((8, 128), 1)
    full_lane = iota((128, 128), 1)
    full_xp = full_lane & 15
    gx = i * 8 + full_xp - 4
    in_x = (gx >= 0) & (gx < NGX * 8)
    for n, ref in enumerate((own, left, right)):
        valid = ((j > 0) if n == 1 else (j < NGY - 1)) if n else (j >= 0)
        colour = jnp.where(lane == 32, jnp.where(valid, 1.0, 0.0) * (ref[48] + 1.0), 0.0) - 1.0
        meta[n * 8 : n * 8 + 8, :] = colour
    fin[0] = left[48] * (j > 0).astype(F32)
    fin[1] = right[48] * (j < NGY - 1).astype(F32)
    for f in range(2):
        fin[2 + f] = above[25 + f, :, 128:256] * (i > 0).astype(F32)
        fin[4 + f] = below[25 + f, :, 128:256] * (i < NGX - 1).astype(F32)
    for f in range(2):
        u[f, 0:PAD, :] = jnp.zeros((PAD, 128), F32)
        u[f, ROWS - PAD : ROWS, :] = jnp.zeros((PAD, 128), F32)
    for part, ref in enumerate((left, own, right)):
        lanes = slice(part * 128, part * 128 + 128)
        rows = slice(PAD + part * 128, PAD + part * 128 + 128)
        gy = (j - 1 + part) * 128
        in_y = (gy >= 0) & (gy < NGY * 128)

        def gather(a):
            slot = a % 2
            for p in range(4):
                for h in range(2):
                    z = 2 * p + h
                    buf[slot, z * 16 : z * 16 + 4, :] = above[a * 4 + p, 4 * h : 4 * h + 4, lanes]
                    buf[slot, z * 16 + 4 : z * 16 + 12, :] = ref[a * 8 + z]
                    buf[slot, z * 16 + 12 : z * 16 + 16, :] = below[a * 4 + p, 4 * h : 4 * h + 4, lanes]
            return buf[slot].T

        stat[0, rows, :] = gather(0)
        stat[1, rows, :] = gather(1)
        stat[2, rows, :] = 0.25 * (gather(2) - 0.125)
        force = [gather(3), gather(4)]
        label = gather(5)
        buf[0] = jnp.zeros((128, 128), F32)
        for z in range(8):
            buf[0, z * 16 : z * 16 + 1, :] = above[24, z : z + 1, lanes]
            buf[0, z * 16 + 15 : z * 16 + 16, :] = below[24, z : z + 1, lanes]
        outer = buf[0].T
        y_ok = in_y.astype(F32)
        out_ok = jnp.where(full_xp == 0, (i > 0).astype(F32), (i < NGX - 1).astype(F32)) * y_ok
        for f in range(2):
            hot = (label == f + 1.0).astype(F32) * (in_x.astype(F32) * y_ok)
            u[f, rows, :] = hot
            stat[3 + f, rows, :] = hot + force[f]
            uo[f, rows, :] = (outer == f + 1.0).astype(F32) * out_ok
    solve_round(0, stat, u, uo, meta, (c0, c1, c2), i, j)
    emit(0, u, out1, out2, even)


def middle_kernel(rnd, stat, u_in, meta, first, second, u, out1, out2, uo, c0, c1, c2):
    i = lax.axis_index("gx")
    j = lax.axis_index("gy")
    u[...] = u_in[...]
    absorb(rnd - 1, u, uo, first, second, i)
    solve_round(rnd, stat, u, uo, meta, (c0, c1, c2), i, j)
    emit(rnd, u, out1, out2, i % 2 == 0)


def last_kernel(stat, u_in, meta, first, second, fin, mix, forc, lab, basis, nat, send, u, uo, c0):
    i = lax.axis_index("gx")
    j = lax.axis_index("gy")
    u[...] = u_in[...]
    absorb(4, u, uo, first, second, i)
    solve_round(5, stat, u, uo, meta, (c0,), i, j)
    sub = iota((8, 128), 0)
    lane = iota((8, 128), 1)
    tiles = []
    for f in range(2):
        flat = u[f, PAD + 128 : PAD + 256, :].T
        for z in range(8):
            tile = flat[z * 16 + 4 : z * 16 + 12, :]
            nat[f, z] = tile
            tiles.append(tile)
    cols = edge_columns(tiles)
    sums = [jnp.zeros((8, 128), F32) for _ in range(10)]
    left = cols * roll(fin[0], -16, 1)
    right = cols * roll(fin[1], 16, 1)
    for f in range(2):
        acc = jnp.zeros((8, 128), F32)
        for z in range(8):
            c, other = tiles[f * 8 + z], tiles[(1 - f) * 8 + z]
            near = jnp.where(sub == 0, 0.0, roll(c, 1, 0)) + jnp.where(sub == 7, 0.0, roll(c, -1, 0))
            near = near + jnp.where(lane == 0, 0.0, roll(c, 1, 1)) + jnp.where(lane == 127, 0.0, roll(c, -1, 1))
            if z > 0:
                near = near + tiles[f * 8 + z - 1]
            if z < 7:
                near = near + tiles[f * 8 + z + 1]
            s12 = 0.25 * (mix[2, z] - 0.125)
            rhs = (lab[z] == f + 1).astype(F32) + forc[f, z]
            acc = acc + basis[f, z] * (rhs - ((mix[f, z] + 6.0) * c + s12 * other - near))
        sums[f] = acc
        top = jnp.zeros((8, 128), F32)
        bot = jnp.zeros((8, 128), F32)
        for z in range(8):
            top = jnp.where(sub == z, jnp.broadcast_to(tiles[f * 8 + z][0:1, :], (8, 128)), top)
            bot = jnp.where(sub == z, jnp.broadcast_to(tiles[f * 8 + z][7:8, :], (8, 128)), bot)
        sums[2 + f] = top * fin[2 + f]
        sums[4 + f] = bot * fin[4 + f]
        sums[6 + f] = jnp.where((lane >= f * 8) & (lane < f * 8 + 8), left, 0.0)
        sums[8 + f] = jnp.where((lane >= 16 + f * 8) & (lane < 24 + f * 8), right, 0.0)
    here = i * NGY + j
    slot = iota((2, 128), 0) * 128 + iota((2, 128), 1)
    row = jnp.zeros((2, 128), F32)
    for n, at in enumerate((here, here - NGY, here + NGY, here - 1, here + 1)):
        for f in range(2):
            total = jnp.sum(sums[2 * n + f], keepdims=True) * (1.0 / 8192.0)
            row = jnp.where(slot == 2 * at + f, total, row)
    send[...] = jnp.broadcast_to(row[None], (NGX * NGY, 2, 128))


def lift_kernel(got, inv, basis, nat, out, coarse):
    q = jnp.sum(got[...], axis=0)
    lane = iota((1, 2), 1)
    pair = jnp.zeros((1, 2), F32)
    for f in range(2):
        c = jnp.sum(q[0:1, :] * inv[0, 0, f : f + 1, 0:128] + q[1:2, :] * inv[0, 0, f : f + 1, 128:256], keepdims=True)
        out[f] = nat[f] + basis[f] * c.reshape(1, 1, 1)
        pair = jnp.where(lane == f, c, pair)
    coarse[0] = pair


def sds(*shape):
    return jax.ShapeDtypeStruct(shape, F32)


def call(kernel, out, scratch=(), **kw):
    return pl.pallas_call(
        kernel,
        out_shape=out,
        scratch_shapes=list(scratch),
        compiler_params=pltpu.CompilerParams(vmem_limit_bytes=48 * 1024 * 1024),
        **kw,
    )


def shift(x, axis, by):
    n = lax.axis_size(axis)
    return lax.ppermute(x, axis, [(k, (k + by) % n) for k in range(n)])


def swap(x, odd):
    n = lax.axis_size("gx")
    return lax.ppermute(x, "gx", [(k, (((k + odd) ^ 1) - odd) % n) for k in range(n)])


def shards(mixing, forcing, labels, colours, coarse_basis, coarse_inverse):
    coef = lambda t: pltpu.VMEM((6, t, 8, 128), F32)
    block = call(
        pack_kernel,
        sds(49, 8, 128),
        [
            pltpu.VMEM((8, 8, 128), jnp.int32),
            pltpu.VMEM((2, 8, 8, 128), F32),
            pltpu.SemaphoreType.DMA((8,)),
        ],
        in_specs=[pl.BlockSpec(memory_space=pltpu.HBM)] * 4 + [pl.BlockSpec(memory_space=pltpu.VMEM)],
        name="pack",
    )(
        *(pltpu.with_memory_space_constraint(x, pltpu.HBM) for x in (mixing, forcing, labels, coarse_basis)),
        jnp.broadcast_to(colours, (8, 128)),
    )
    left = shift(block, "gy", 1)
    right = shift(block, "gy", -1)
    one, two = call(rows_kernel, (sds(27, 8, 384), sds(27, 8, 384)), name="rows")(block, left, right, coarse_basis)
    one, two = swap(one, 0), swap(two, 1)
    msg = lambda r: sds(8 * len(message_items(r)), 128)
    stat, u, meta, fin, one, two = call(
        start_kernel,
        (sds(5, ROWS, 128), sds(2, ROWS, 128), sds(24, 128), sds(6, 8, 128), msg(0), msg(0)),
        [pltpu.VMEM((2, 27, 8, 384), F32), pltpu.VMEM((2, 128, 128), F32), pltpu.VMEM((2, ROWS, 128), F32)]
        + [coef(17), coef(16), coef(16)],
        name="round0",
    )(block, left, right, one, two)
    for rnd in range(1, 5):
        one, two = swap(one, 0), swap(two, 1)
        u, one, two = call(
            lambda *refs, rnd=rnd: middle_kernel(rnd, *refs),
            (sds(2, ROWS, 128), msg(rnd), msg(rnd)),
            [pltpu.VMEM((2, ROWS, 128), F32), coef(17), coef(16), coef(16)],
            name=f"round{rnd}",
        )(stat, u, meta, one, two)
    one, two = swap(one, 0), swap(two, 1)
    nat, send = call(
        last_kernel,
        (sds(2, 8, 8, 128), sds(NGX * NGY, 2, 128)),
        [pltpu.VMEM((2, ROWS, 128), F32), pltpu.VMEM((2, ROWS, 128), F32), coef(17)],
        name="round5",
    )(stat, u, meta, one, two, fin, mixing, forcing, labels, coarse_basis)
    got = lax.all_to_all(send, ("gx", "gy"), 0, 0, tiled=True)
    return call(lift_kernel, (sds(2, 8, 8, 128), sds(1, 1, 2)), name="lift")(got, coarse_inverse, coarse_basis, nat)


def solution(mesh):
    return jax.shard_map(
        shards,
        mesh=mesh,
        in_specs=(
            P(None, None, "gx", "gy"),
            P(None, None, "gx", "gy"),
            P(None, "gx", "gy"),
            P("gx", "gy"),
            P(None, None, "gx", "gy"),
            P("gx", "gy", None, None),
        ),
        out_specs=(P(None, None, "gx", "gy"), P("gx", "gy", None)),
        check_vma=False,
    )
```

profile of v0, /device:TPU:1, one launch (start us, length us, event | category | flops | bytes accessed | tf_op | source)
XLA Modules:
  0.0 102.6 jit_solution(4599889105762646812)
XLA Ops:
  1.3 1.1 %pack.1.own = f32[49,8,128]{2,1,0:T(8,128)S(1)} custom-call(f32[3,8,8,128]{3,2,1,0:T(8,128)} %mix.3, f32[2,8,8,128]{3,2,1,0:T(8,128)} %forc.3, s32[8,8,128]{2,1,0:T(8,128)} %lab.3, f32[2,8,8,128]{3,2,1,0:T(8,128)} %basis.7, s32[8,128]{1,0:T(8,128)S(1)} %broadcast_in_dim.8.colour), custom_call_target="tpu_custom_call" | custom-call | tf_op jit(solution)/shard_map/pack/pallas_call | solution.py:412
  2.4 5.6 %collective-permute-start.1 = (f32[49,8,128]{2,1,0:T(8,128)S(1)}, f32[49,8,128]{2,1,0:T(8,128)S(1)}, u32[]{:S(2)}, u32[]{:S(2)}) collective-permute-start(f32[49,8,128]{2,1,0:T(8,128)S(1)} %pack.1.own), channel_id=1, source_target_pairs={{0,7},{1,0},{2,1},{3,2},{4,3},{5,4},{6,5},{7,6},{8,15},{9,8},{10,9... | collective-permute-start | bytes 602120 | tf_op jit(solution)/shard_map/ppermute | solution.py:402
  8.0 3.7 %collective-permute-done.1.right = f32[49,8,128]{2,1,0:T(8,128)S(1)} collective-permute-done((f32[49,8,128]{2,1,0:T(8,128)S(1)}, f32[49,8,128]{2,1,0:T(8,128)S(1)}, u32[]{:S(2)}, u32[]{:S(2)}) %collective-permute-start.1) | collective-permute-done | bytes 200736 | tf_op jit(solution)/shard_map/ppermute | solution.py:402
  11.6 4.0 %collective-permute-done.left = f32[49,8,128]{2,1,0:T(8,128)S(1)} collective-permute-done((f32[49,8,128]{2,1,0:T(8,128)S(1)}, f32[49,8,128]{2,1,0:T(8,128)S(1)}, u32[]{:S(2)}, u32[]{:S(2)}) %collective-permute-start) | collective-permute-done | bytes 200736 | tf_op jit(solution)/shard_map/ppermute | solution.py:402
  15.7 1.9 %collective-permute-start.2 = (f32[27,8,384]{2,1,0:T(8,128)S(1)}, f32[27,8,384]{2,1,0:T(8,128)S(1)}, u32[]{:S(2)}, u32[]{:S(2)}) collective-permute-start(f32[27,8,384]{2,1,0:T(8,128)S(1)} %get-tuple-element.24), channel_id=1, source_target_pairs={{0,8},{8,0},{16,24},{24,16},{32,40},{40,32},{48,56},{56,48},{64,72... | collective-permute-start | bytes 995336 | tf_op jit(solution)/shard_map/ppermute | solution.py:407
  17.7 2.4 %collective-permute-start.3 = (f32[27,8,384]{2,1,0:T(8,128)S(1)}, f32[27,8,384]{2,1,0:T(8,128)S(1)}, u32[]{:S(2)}, u32[]{:S(2)}) collective-permute-start(f32[27,8,384]{2,1,0:T(8,128)S(1)} %get-tuple-element.25), channel_id=1, source_target_pairs={{0,120},{8,16},{16,8},{24,32},{32,24},{40,48},{48,40},{56,64},{64,... | collective-permute-start | bytes 995336 | tf_op jit(solution)/shard_map/ppermute | solution.py:407
  20.1 9.1 %collective-permute-done.3.second = f32[27,8,384]{2,1,0:T(8,128)S(1)} collective-permute-done((f32[27,8,384]{2,1,0:T(8,128)S(1)}, f32[27,8,384]{2,1,0:T(8,128)S(1)}, u32[]{:S(2)}, u32[]{:S(2)}) %collective-permute-start.3) | collective-permute-done | bytes 331808 | tf_op jit(solution)/shard_map/ppermute | solution.py:407
  29.2 0.9 round0.1
  30.1 4.1 %collective-permute-start.4 = (f32[224,128]{1,0:T(8,128)S(1)}, f32[224,128]{1,0:T(8,128)S(1)}, u32[]{:S(2)}, u32[]{:S(2)}) collective-permute-start(f32[224,128]{1,0:T(8,128)S(1)} %get-tuple-element.29), channel_id=1, source_target_pairs={{0,8},{8,0},{16,24},{24,16},{32,40},{40,32},{48,56},{56,48},{64,72... | collective-permute-start | bytes 344072 | tf_op jit(solution)/shard_map/ppermute | solution.py:407
  34.2 4.8 %collective-permute-start.5 = (f32[224,128]{1,0:T(8,128)S(1)}, f32[224,128]{1,0:T(8,128)S(1)}, u32[]{:S(2)}, u32[]{:S(2)}) collective-permute-start(f32[224,128]{1,0:T(8,128)S(1)} %get-tuple-element.30), channel_id=1, source_target_pairs={{0,120},{8,16},{16,8},{24,32},{32,24},{40,48},{48,40},{56,64},{64,... | collective-permute-start | bytes 344072 | tf_op jit(solution)/shard_map/ppermute | solution.py:407
  39.0 3.4 %collective-permute-done.5.refs_4_ = f32[224,128]{1,0:T(8,128)S(1)} collective-permute-done((f32[224,128]{1,0:T(8,128)S(1)}, f32[224,128]{1,0:T(8,128)S(1)}, u32[]{:S(2)}, u32[]{:S(2)}) %collective-permute-start.5) | collective-permute-done | bytes 114720 | tf_op jit(solution)/shard_map/ppermute | solution.py:407
  42.4 3.7 %round1.1 = (f32[2,400,128]{2,1,0:T(8,128)S(1)}, f32[192,128]{1,0:T(8,128)S(1)}, f32[192,128]{1,0:T(8,128)S(1)}) custom-call(f32[5,400,128]{2,1,0:T(8,128)S(1)} %get-tuple-element.26.refs_0_.stat, f32[2,400,128]{2,1,0:T(8,128)S(1)} %get-tuple-element.27.refs_1_, f32[24,128]{1,0:T(8,128)S(1)} %get-tuple-element.28.refs_2_.meta, ...), custom_call_target="tpu_custom_call" | custom-call | tf_op jit(solution)/shard_map/round1/pallas_call | solution.py:440
  46.1 0.1 collective-permute-start.6
  46.2 0.6 collective-permute-start.7
  46.8 0.7 collective-permute-done.6.refs_3_
  47.5 4.3 %collective-permute-done.7.refs_4_ = f32[192,128]{1,0:T(8,128)S(1)} collective-permute-done((f32[192,128]{1,0:T(8,128)S(1)}, f32[192,128]{1,0:T(8,128)S(1)}, u32[]{:S(2)}, u32[]{:S(2)}) %collective-permute-start.7) | collective-permute-done | bytes 98336 | tf_op jit(solution)/shard_map/ppermute | solution.py:407
  51.8 3.4 %round2.1 = (f32[2,400,128]{2,1,0:T(8,128)S(1)}, f32[160,128]{1,0:T(8,128)S(1)}, f32[160,128]{1,0:T(8,128)S(1)}) custom-call(f32[5,400,128]{2,1,0:T(8,128)S(1)} %get-tuple-element.26.refs_0_.stat, f32[2,400,128]{2,1,0:T(8,128)S(1)} %get-tuple-element.31.refs_1_, f32[24,128]{1,0:T(8,128)S(1)} %get-tuple-element.28.refs_2_.meta, ...), custom_call_target="tpu_custom_call" | custom-call | tf_op jit(solution)/shard_map/round2/pallas_call | solution.py:440
  55.2 0.1 collective-permute-start.8
  55.3 0.1 collective-permute-start.9
  55.4 1.2 %collective-permute-done.8.refs_3_ = f32[160,128]{1,0:T(8,128)S(1)} collective-permute-done((f32[160,128]{1,0:T(8,128)S(1)}, f32[160,128]{1,0:T(8,128)S(1)}, u32[]{:S(2)}, u32[]{:S(2)}) %collective-permute-start.8) | collective-permute-done | bytes 81952 | tf_op jit(solution)/shard_map/ppermute | solution.py:407
  56.6 4.2 %collective-permute-done.9.refs_4_ = f32[160,128]{1,0:T(8,128)S(1)} collective-permute-done((f32[160,128]{1,0:T(8,128)S(1)}, f32[160,128]{1,0:T(8,128)S(1)}, u32[]{:S(2)}, u32[]{:S(2)}) %collective-permute-start.9) | collective-permute-done | bytes 81952 | tf_op jit(solution)/shard_map/ppermute | solution.py:407
  60.7 0.9 round3.1
  61.6 3.1 %collective-permute-start.10 = (f32[128,128]{1,0:T(8,128)S(1)}, f32[128,128]{1,0:T(8,128)S(1)}, u32[]{:S(2)}, u32[]{:S(2)}) collective-permute-start(f32[128,128]{1,0:T(8,128)S(1)} %get-tuple-element.38), channel_id=1, source_target_pairs={{0,8},{8,0},{16,24},{24,16},{32,40},{40,32},{48,56},{56,48},{64,72... | collective-permute-start | bytes 196616 | tf_op jit(solution)/shard_map/ppermute | solution.py:407
  64.7 0.9 collective-permute-done.10.refs_3_
  65.6 4.3 %collective-permute-done.11.refs_4_ = f32[128,128]{1,0:T(8,128)S(1)} collective-permute-done((f32[128,128]{1,0:T(8,128)S(1)}, f32[128,128]{1,0:T(8,128)S(1)}, u32[]{:S(2)}, u32[]{:S(2)}) %collective-permute-start.11) | collective-permute-done | bytes 65568 | tf_op jit(solution)/shard_map/ppermute | solution.py:407
  69.9 0.6 round4.1
  70.5 2.4 %collective-permute-start.12 = (f32[96,128]{1,0:T(8,128)S(1)}, f32[96,128]{1,0:T(8,128)S(1)}, u32[]{:S(2)}, u32[]{:S(2)}) collective-permute-start(f32[96,128]{1,0:T(8,128)S(1)} %get-tuple-element.41), channel_id=1, source_target_pairs={{0,8},{8,0},{16,24},{24,16},{32,40},{40,32},{48,56},{56,48},{64,72... | collective-permute-start | bytes 147464 | tf_op jit(solution)/shard_map/ppermute | solution.py:407
  73.0 0.9 collective-permute-done.12.first
  73.8 4.1 %collective-permute-done.13.second = f32[96,128]{1,0:T(8,128)S(1)} collective-permute-done((f32[96,128]{1,0:T(8,128)S(1)}, f32[96,128]{1,0:T(8,128)S(1)}, u32[]{:S(2)}, u32[]{:S(2)}) %collective-permute-start.13) | collective-permute-done | bytes 49184 | tf_op jit(solution)/shard_map/ppermute | solution.py:407
  78.0 0.7 round5.1
  78.7 23.0 %all_to_all.5.got = f32[128,2,128]{2,1,0:T(2,128)S(1)} all-to-all(f32[128,2,128]{2,1,0:T(2,128)S(1)} %get-tuple-element.44), channel_id=1, replica_groups=mesh['gx'=16,'gy'=8] {'gx','gy'}, dimensions={0} | all-to-all | bytes 262144 | tf_op jit(solution)/shard_map/all_to_all | solution.py:453
  101.7 0.9 lift.1
  (17 shorter events, 0.1 us)
Async XLA Ops:
  1.3 14.3 %copy-start = (f32[2,8,8,128]{3,2,1,0:T(8,128)S(1)}, f32[2,8,8,128]{3,2,1,0:T(8,128)}, u32[]{:S(2)}) copy-start(f32[2,8,8,128]{3,2,1,0:T(8,128)} %basis.7) | copy-start | bytes 196612
  2.4 9.2 %collective-permute-start.1 = (f32[49,8,128]{2,1,0:T(8,128)S(1)}, f32[49,8,128]{2,1,0:T(8,128)S(1)}, u32[]{:S(2)}, u32[]{:S(2)}) collective-permute-start(f32[49,8,128]{2,1,0:T(8,128)S(1)} %pack.1.own), channel_id=1, source_target_pairs={{0,7},{1,0},{2,1},{3,2},{4,3},{5,4},{6,5},{7,6},{8,15},{9,8},{10,9... | collective-permute-start | bytes 602120 | tf_op jit(solution)/shard_map/ppermute | solution.py:402
  8.0 7.6 %collective-permute-start = (f32[49,8,128]{2,1,0:T(8,128)S(1)}, f32[49,8,128]{2,1,0:T(8,128)S(1)}, u32[]{:S(2)}, u32[]{:S(2)}) collective-permute-start(f32[49,8,128]{2,1,0:T(8,128)S(1)} %pack.1.own), channel_id=1, source_target_pairs={{0,1},{1,2},{2,3},{3,4},{4,5},{5,6},{6,7},{7,0},{8,9},{9,10},{10,1... | collective-permute-start | bytes 602120 | tf_op jit(solution)/shard_map/ppermute | solution.py:402
  15.7 4.4 %collective-permute-start.2 = (f32[27,8,384]{2,1,0:T(8,128)S(1)}, f32[27,8,384]{2,1,0:T(8,128)S(1)}, u32[]{:S(2)}, u32[]{:S(2)}) collective-permute-start(f32[27,8,384]{2,1,0:T(8,128)S(1)} %get-tuple-element.24), channel_id=1, source_target_pairs={{0,8},{8,0},{16,24},{24,16},{32,40},{40,32},{48,56},{56,48},{64,72... | collective-permute-start | bytes 995336 | tf_op jit(solution)/shard_map/ppermute | solution.py:407
  17.7 11.6 %collective-permute-start.3 = (f32[27,8,384]{2,1,0:T(8,128)S(1)}, f32[27,8,384]{2,1,0:T(8,128)S(1)}, u32[]{:S(2)}, u32[]{:S(2)}) collective-permute-start(f32[27,8,384]{2,1,0:T(8,128)S(1)} %get-tuple-element.25), channel_id=1, source_target_pairs={{0,120},{8,16},{16,8},{24,32},{32,24},{40,48},{48,40},{56,64},{64,... | collective-permute-start | bytes 995336 | tf_op jit(solution)/shard_map/ppermute | solution.py:407
  30.1 8.9 %collective-permute-start.4 = (f32[224,128]{1,0:T(8,128)S(1)}, f32[224,128]{1,0:T(8,128)S(1)}, u32[]{:S(2)}, u32[]{:S(2)}) collective-permute-start(f32[224,128]{1,0:T(8,128)S(1)} %get-tuple-element.29), channel_id=1, source_target_pairs={{0,8},{8,0},{16,24},{24,16},{32,40},{40,32},{48,56},{56,48},{64,72... | collective-permute-start | bytes 344072 | tf_op jit(solution)/shard_map/ppermute | solution.py:407
  34.2 8.2 %collective-permute-start.5 = (f32[224,128]{1,0:T(8,128)S(1)}, f32[224,128]{1,0:T(8,128)S(1)}, u32[]{:S(2)}, u32[]{:S(2)}) collective-permute-start(f32[224,128]{1,0:T(8,128)S(1)} %get-tuple-element.30), channel_id=1, source_target_pairs={{0,120},{8,16},{16,8},{24,32},{32,24},{40,48},{48,40},{56,64},{64,... | collective-permute-start | bytes 344072 | tf_op jit(solution)/shard_map/ppermute | solution.py:407
  46.1 1.4 %collective-permute-start.6 = (f32[192,128]{1,0:T(8,128)S(1)}, f32[192,128]{1,0:T(8,128)S(1)}, u32[]{:S(2)}, u32[]{:S(2)}) collective-permute-start(f32[192,128]{1,0:T(8,128)S(1)} %get-tuple-element.32), channel_id=1, source_target_pairs={{0,8},{8,0},{16,24},{24,16},{32,40},{40,32},{48,56},{56,48},{64,72... | collective-permute-start | bytes 294920 | tf_op jit(solution)/shard_map/ppermute | solution.py:407
  46.2 5.6 %collective-permute-start.7 = (f32[192,128]{1,0:T(8,128)S(1)}, f32[192,128]{1,0:T(8,128)S(1)}, u32[]{:S(2)}, u32[]{:S(2)}) collective-permute-start(f32[192,128]{1,0:T(8,128)S(1)} %get-tuple-element.33), channel_id=1, source_target_pairs={{0,120},{8,16},{16,8},{24,32},{32,24},{40,48},{48,40},{56,64},{64,... | collective-permute-start | bytes 294920 | tf_op jit(solution)/shard_map/ppermute | solution.py:407
  55.2 1.4 %collective-permute-start.8 = (f32[160,128]{1,0:T(8,128)S(1)}, f32[160,128]{1,0:T(8,128)S(1)}, u32[]{:S(2)}, u32[]{:S(2)}) collective-permute-start(f32[160,128]{1,0:T(8,128)S(1)} %get-tuple-element.35), channel_id=1, source_target_pairs={{0,8},{8,0},{16,24},{24,16},{32,40},{40,32},{48,56},{56,48},{64,72... | collective-permute-start | bytes 245768 | tf_op jit(solution)/shard_map/ppermute | solution.py:407
  55.3 5.5 %collective-permute-start.9 = (f32[160,128]{1,0:T(8,128)S(1)}, f32[160,128]{1,0:T(8,128)S(1)}, u32[]{:S(2)}, u32[]{:S(2)}) collective-permute-start(f32[160,128]{1,0:T(8,128)S(1)} %get-tuple-element.36), channel_id=1, source_target_pairs={{0,120},{8,16},{16,8},{24,32},{32,24},{40,48},{48,40},{56,64},{64,... | collective-permute-start | bytes 245768 | tf_op jit(solution)/shard_map/ppermute | solution.py:407
  61.6 4.0 %collective-permute-start.10 = (f32[128,128]{1,0:T(8,128)S(1)}, f32[128,128]{1,0:T(8,128)S(1)}, u32[]{:S(2)}, u32[]{:S(2)}) collective-permute-start(f32[128,128]{1,0:T(8,128)S(1)} %get-tuple-element.38), channel_id=1, source_target_pairs={{0,8},{8,0},{16,24},{24,16},{32,40},{40,32},{48,56},{56,48},{64,72... | collective-permute-start | bytes 196616 | tf_op jit(solution)/shard_map/ppermute | solution.py:407
  64.7 5.2 %collective-permute-start.11 = (f32[128,128]{1,0:T(8,128)S(1)}, f32[128,128]{1,0:T(8,128)S(1)}, u32[]{:S(2)}, u32[]{:S(2)}) collective-permute-start(f32[128,128]{1,0:T(8,128)S(1)} %get-tuple-element.39), channel_id=1, source_target_pairs={{0,120},{8,16},{16,8},{24,32},{32,24},{40,48},{48,40},{56,64},{64,... | collective-permute-start | bytes 196616 | tf_op jit(solution)/shard_map/ppermute | solution.py:407
  69.9 8.0 %copy-start.1 = (f32[3,8,8,128]{3,2,1,0:T(8,128)S(1)}, f32[3,8,8,128]{3,2,1,0:T(8,128)}, u32[]{:S(2)}) copy-start(f32[3,8,8,128]{3,2,1,0:T(8,128)} %mix.3) | copy-start | bytes 294916
  69.9 8.0 %copy-start.2 = (f32[2,8,8,128]{3,2,1,0:T(8,128)S(1)}, f32[2,8,8,128]{3,2,1,0:T(8,128)}, u32[]{:S(2)}) copy-start(f32[2,8,8,128]{3,2,1,0:T(8,128)} %forc.3) | copy-start | bytes 196612
  69.9 8.0 %copy-start.3 = (s32[8,8,128]{2,1,0:T(8,128)S(1)}, s32[8,8,128]{2,1,0:T(8,128)}, u32[]{:S(2)}) copy-start(s32[8,8,128]{2,1,0:T(8,128)} %lab.3) | copy-start | bytes 98308
  70.5 3.3 %collective-permute-start.12 = (f32[96,128]{1,0:T(8,128)S(1)}, f32[96,128]{1,0:T(8,128)S(1)}, u32[]{:S(2)}, u32[]{:S(2)}) collective-permute-start(f32[96,128]{1,0:T(8,128)S(1)} %get-tuple-element.41), channel_id=1, source_target_pairs={{0,8},{8,0},{16,24},{24,16},{32,40},{40,32},{48,56},{56,48},{64,72... | collective-permute-start | bytes 147464 | tf_op jit(solution)/shard_map/ppermute | solution.py:407
  73.0 5.0 %collective-permute-start.13 = (f32[96,128]{1,0:T(8,128)S(1)}, f32[96,128]{1,0:T(8,128)S(1)}, u32[]{:S(2)}, u32[]{:S(2)}) collective-permute-start(f32[96,128]{1,0:T(8,128)S(1)} %get-tuple-element.42), channel_id=1, source_target_pairs={{0,120},{8,16},{16,8},{24,32},{32,24},{40,48},{48,40},{56,64},{64,... | collective-permute-start | bytes 147464 | tf_op jit(solution)/shard_map/ppermute | solution.py:407
  78.7 23.0 %copy-start.4 = (f32[1,1,2,256]{3,2,1,0:T(2,128)S(1)}, f32[1,1,2,256]{3,2,1,0:T(2,128)}, u32[]{:S(2)}) copy-start(f32[1,1,2,256]{3,2,1,0:T(2,128)} %inv.1) | copy-start | bytes 6148
where the time goes:
time: 102 us; the launch traced here: 103 us
  waiting for transfers between devices  40.8 us (40%)
  starting transfers between devices  25.3 us (25%)
  blocking collectives  23 us (23%)
  Pallas kernels  12.1 us (12%)
  between operations  1.4 us (1%)
    ppermute x12, waiting for transfers between devices, swap(): lax.ppermute(x, 'gx', [(k, ((k + odd ^ 1) - odd) % n) for k in range(n)])  33.1 us
    all_to_all x1, blocking collectives, shards(): got = lax.all_to_all(send, ('gx', 'gy'), 0, 0, tiled=True)  23 us
    ppermute x12, starting transfers between devices, swap(): lax.ppermute(x, 'gx', [(k, ((k + odd ^ 1) - odd) % n) for k in range(n)])  19.7 us
    pallas_call x4, Pallas kernels, shards(): call(lambda *refs, rnd=rnd: middle_kernel(rnd, *refs), (sds(2, ROWS, 128)...  8.45 us
    ppermute x2, waiting for transfers between devices, shift(): return lax.ppermute(x, axis, [(k, (k + by) % n) for k in range(n)])  7.65 us
    ppermute x2, starting transfers between devices, shift(): return lax.ppermute(x, axis, [(k, (k + by) % n) for k in range(n)])  5.59 us
  transfers between devices with their start and end apart: 14, of which 12 were waited for; matrix products, arithmetic and copies ran while one was open for 0% of the time, Pallas kernels for 0%

commit v1 on v0

--- a/solution.py
+++ b/solution.py
@@ -17,6 +17,24 @@
 NGY = 8
 
 
+def home(i, j):
+    pair, core = i // 2, i % 2
+    y, low = (pair, 0) if pair < 4 else (7 - pair, 1)
+    return (y * 4 + j // 4 * 2 + core) * NGY + low * 4 + j % 4
+
+
+def block_here():
+    gx, gy = lax.axis_index("gx"), lax.axis_index("gy")
+    y, low = gx // 4, gy // 4
+    pair = jnp.where(low == 0, y, 7 - y)
+    return pair * 2 + gx % 2, gx // 2 % 2 * 4 + gy % 4
+
+
+def send(x, to):
+    blocks = [(i, j) for i in range(NGX) for j in range(NGY)]
+    return lax.ppermute(x, ("gx", "gy"), [to(i, j) for i, j in blocks])
+
+
 def iota(shape, dim):
     return lax.broadcasted_iota(jnp.int32, shape, dim)
 
@@ -40,10 +58,11 @@
     return out
 
 
-def pack_kernel(mix, forc, lab, basis, colour, out, lab_v, basis_v, sems):
+def pack_kernel(mix, forc, lab, basis, colour, out, full, lab_v, sems):
     copies = [
-        pltpu.make_async_copy(basis, basis_v, sems.at[0]),
-        pltpu.make_async_copy(lab, lab_v, sems.at[1]),
+        pltpu.make_async_copy(lab, lab_v, sems.at[0]),
+        pltpu.make_async_copy(basis.at[0], full.at[pl.ds(49, 8)], sems.at[1]),
+        pltpu.make_async_copy(basis.at[1], full.at[pl.ds(57, 8)], sems.at[2]),
     ]
     for f in range(3):
         copies.append(pltpu.make_async_copy(mix.at[f], out.at[pl.ds(f * 8, 8)], sems.at[3 + f]))
@@ -54,18 +73,19 @@
     for c in copies:
         c.wait()
     out[40:48] = lab_v[...].astype(F32)
-    cols = edge_columns([basis_v[f, z] for f in range(2) for z in range(8)])
+    cols = edge_columns([full[49 + n] for n in range(16)])
     lane = iota((8, 128), 1)
     out[48] = jnp.where(lane == 32, colour[...].astype(F32), cols)
-
-
-def rows_kernel(own, left, right, basis, first, second):
-    even = lax.axis_index("gx") % 2 == 0
-    pl.when(even)(lambda: write_rows(own, left, right, basis, second, first))
-    pl.when(jnp.logical_not(even))(lambda: write_rows(own, left, right, basis, first, second))
-
-
-def write_rows(own, left, right, basis, up, down):
+    full[0:49] = out[...]
+
+
+def rows_kernel(own, left, right, first, second):
+    even = block_here()[0] % 2 == 0
+    pl.when(even)(lambda: write_rows(own, left, right, second, first))
+    pl.when(jnp.logical_not(even))(lambda: write_rows(own, left, right, first, second))
+
+
+def write_rows(own, left, right, up, down):
     for part, ref in enumerate((left, own, right)):
         lanes = slice(part * 128, part * 128 + 128)
         for a in range(6):
@@ -79,8 +99,8 @@
             down[24, z : z + 1, lanes] = ref[40 + z, 3:4, :]
             for f in range(2):
                 if part == 1:
-                    up[25 + f, z : z + 1, lanes] = basis[f, z, 0:1, :]
-                    down[25 + f, z : z + 1, lanes] = basis[f, z, 7:8, :]
+                    up[25 + f, z : z + 1, lanes] = own[49 + f * 8 + z, 0:1, :]
+                    down[25 + f, z : z + 1, lanes] = own[49 + f * 8 + z, 7:8, :]
         if part != 1:
             up[25:27, :, lanes] = jnp.zeros((2, 8, 128), F32)
             down[25:27, :, lanes] = jnp.zeros((2, 8, 128), F32)
@@ -245,7 +265,7 @@
 
 
 def start_kernel(own, left, right, first, second, stat, u, meta, fin, out1, out2, near, buf, uo, c0, c1, c2):
-    i = lax.axis_index("gx")
+    i, j = block_here()
     even = i % 2 == 0
 
     def place(above, below):
@@ -255,7 +275,6 @@
     pl.when(even)(lambda: place(second, first))
     pl.when(jnp.logical_not(even))(lambda: place(first, second))
     above, below = near.at[0], near.at[1]
-    j = lax.axis_index("gy")
     xp, _ = lane_ids()
     lane = iota((8, 128), 1)
     full_lane = iota((128, 128), 1)
@@ -312,17 +331,15 @@
 
 
 def middle_kernel(rnd, stat, u_in, meta, first, second, u, out1, out2, uo, c0, c1, c2):
-    i = lax.axis_index("gx")
-    j = lax.axis_index("gy")
+    i, j = block_here()
     u[...] = u_in[...]
     absorb(rnd - 1, u, uo, first, second, i)
     solve_round(rnd, stat, u, uo, meta, (c0, c1, c2), i, j)
     emit(rnd, u, out1, out2, i % 2 == 0)
 
 
-def last_kernel(stat, u_in, meta, first, second, fin, mix, forc, lab, basis, nat, send, u, uo, c0):
-    i = lax.axis_index("gx")
-    j = lax.axis_index("gy")
+def last_kernel(stat, u_in, meta, first, second, fin, own, nat, rows, u, uo, c0):
+    i, j = block_here()
     u[...] = u_in[...]
     absorb(4, u, uo, first, second, i)
     solve_round(5, stat, u, uo, meta, (c0,), i, j)
@@ -349,9 +366,9 @@
                 near = near + tiles[f * 8 + z - 1]
             if z < 7:
                 near = near + tiles[f * 8 + z + 1]
-            s12 = 0.25 * (mix[2, z] - 0.125)
-            rhs = (lab[z] == f + 1).astype(F32) + forc[f, z]
-            acc = acc + basis[f, z] * (rhs - ((mix[f, z] + 6.0) * c + s12 * other - near))
+            s12 = 0.25 * (own[16 + z] - 0.125)
+            rhs = (own[40 + z] == f + 1.0).astype(F32) + own[24 + f * 8 + z]
+            acc = acc + own[49 + f * 8 + z] * (rhs - ((own[f * 8 + z] + 6.0) * c + s12 * other - near))
         sums[f] = acc
         top = jnp.zeros((8, 128), F32)
         bot = jnp.zeros((8, 128), F32)
@@ -369,7 +386,7 @@
         for f in range(2):
             total = jnp.sum(sums[2 * n + f], keepdims=True) * (1.0 / 8192.0)
             row = jnp.where(slot == 2 * at + f, total, row)
-    send[...] = jnp.broadcast_to(row[None], (NGX * NGY, 2, 128))
+    rows[...] = jnp.broadcast_to(row[None], (NGX * NGY, 2, 128))
 
 
 def lift_kernel(got, inv, basis, nat, out, coarse):
@@ -397,24 +414,17 @@
     )
 
 
-def shift(x, axis, by):
-    n = lax.axis_size(axis)
-    return lax.ppermute(x, axis, [(k, (k + by) % n) for k in range(n)])
-
-
 def swap(x, odd):
-    n = lax.axis_size("gx")
-    return lax.ppermute(x, "gx", [(k, (((k + odd) ^ 1) - odd) % n) for k in range(n)])
+    return send(x, lambda i, j: (home(i, j), home((((i + odd) ^ 1) - odd) % NGX, j)))
 
 
 def shards(mixing, forcing, labels, colours, coarse_basis, coarse_inverse):
     coef = lambda t: pltpu.VMEM((6, t, 8, 128), F32)
-    block = call(
+    block, full = call(
         pack_kernel,
-        sds(49, 8, 128),
+        (sds(49, 8, 128), sds(65, 8, 128)),
         [
             pltpu.VMEM((8, 8, 128), jnp.int32),
-            pltpu.VMEM((2, 8, 8, 128), F32),
             pltpu.SemaphoreType.DMA((8,)),
         ],
         in_specs=[pl.BlockSpec(memory_space=pltpu.HBM)] * 4 + [pl.BlockSpec(memory_space=pltpu.VMEM)],
@@ -423,9 +433,10 @@
         *(pltpu.with_memory_space_constraint(x, pltpu.HBM) for x in (mixing, forcing, labels, coarse_basis)),
         jnp.broadcast_to(colours, (8, 128)),
     )
-    left = shift(block, "gy", 1)
-    right = shift(block, "gy", -1)
-    one, two = call(rows_kernel, (sds(27, 8, 384), sds(27, 8, 384)), name="rows")(block, left, right, coarse_basis)
+    own = send(full, lambda i, j: (i * NGY + j, home(i, j)))
+    left = send(block, lambda i, j: (i * NGY + j, home(i, (j + 1) % NGY)))
+    right = send(block, lambda i, j: (i * NGY + j, home(i, (j - 1) % NGY)))
+    one, two = call(rows_kernel, (sds(27, 8, 384), sds(27, 8, 384)), name="rows")(own, left, right)
     one, two = swap(one, 0), swap(two, 1)
     msg = lambda r: sds(8 * len(message_items(r)), 128)
     stat, u, meta, fin, one, two = call(
@@ -434,7 +445,7 @@
         [pltpu.VMEM((2, 27, 8, 384), F32), pltpu.VMEM((2, 128, 128), F32), pltpu.VMEM((2, ROWS, 128), F32)]
         + [coef(17), coef(16), coef(16)],
         name="round0",
-    )(block, left, right, one, two)
+    )(own, left, right, one, two)
     for rnd in range(1, 5):
         one, two = swap(one, 0), swap(two, 1)
         u, one, two = call(
@@ -444,13 +455,14 @@
             name=f"round{rnd}",
         )(stat, u, meta, one, two)
     one, two = swap(one, 0), swap(two, 1)
-    nat, send = call(
+    nat, rows = call(
         last_kernel,
         (sds(2, 8, 8, 128), sds(NGX * NGY, 2, 128)),
         [pltpu.VMEM((2, ROWS, 128), F32), pltpu.VMEM((2, ROWS, 128), F32), coef(17)],
         name="round5",
-    )(stat, u, meta, one, two, fin, mixing, forcing, labels, coarse_basis)
-    got = lax.all_to_all(send, ("gx", "gy"), 0, 0, tiled=True)
+    )(stat, u, meta, one, two, fin, own)
+    nat = send(nat, lambda i, j: (home(i, j), i * NGY + j))
+    got = lax.all_to_all(rows, ("gx", "gy"), 0, 0, tiled=True)
     return call(lift_kernel, (sds(2, 8, 8, 128), sds(1, 1, 2)), name="lift")(got, coarse_inverse, coarse_basis, nat)
 
 

time: 102 us -> 97.4 us (0.955); the launches traced: 103 us -> 96 us
  blocking collectives: 23 us -> 0 us
  starting transfers between devices: 25.3 us -> 47.2 us
  waiting for transfers between devices: 40.8 us -> 37.3 us
  Pallas kernels: 12.1 us -> 10.1 us
    all_to_all x1 -> x0, blocking collectives: 23 us -> none  [shards(): got = lax.all_to_all(send, ('gx', 'gy'), 0, 0, tiled=True)]
    ppermute x14 -> x16, waiting for transfers between devices: 40.8 us -> 28 us  [send(): return lax.ppermute(x, ('gx', 'gy'), [to(i, j) for i, j in blocks])]
    all_to_all x0 -> x1, starting transfers between devices: none -> 12 us  [shards(): got = lax.all_to_all(rows, ('gx', 'gy'), 0, 0, tiled=True)]
    ppermute x14 -> x16, starting transfers between devices: 25.3 us -> 35.2 us  [send(): return lax.ppermute(x, ('gx', 'gy'), [to(i, j) for i, j in blocks])]
    all_to_all x0 -> x1, waiting for transfers between devices: none -> 9.32 us  [shards(): got = lax.all_to_all(rows, ('gx', 'gy'), 0, 0, tiled=True)]
    pallas_call x4, Pallas kernels: 8.45 us -> 5.84 us  [shards(): call(lambda *refs, rnd=rnd: middle_kernel(rnd, *refs), (sds(2, ROWS, 128)...]
  transfers between devices with their start and end apart: 14 -> 17, of which waited for: 12 -> 12; matrix products, arithmetic and copies ran while one was open for 0% -> 0% of each run, Pallas kernels for 0% -> 0%
where the time goes in v1:
time: 97.4 us; the launch traced here: 96 us
  starting transfers between devices  47.2 us (48%)
  waiting for transfers between devices  37.3 us (38%)
  Pallas kernels  10.1 us (10%)
  between operations  1.41 us (1%)
    ppermute x16, starting transfers between devices, send(): return lax.ppermute(x, ('gx', 'gy'), [to(i, j) for i, j in blocks])  35.2 us
    ppermute x16, waiting for transfers between devices, send(): return lax.ppermute(x, ('gx', 'gy'), [to(i, j) for i, j in blocks])  28 us
    all_to_all x1, starting transfers between devices, shards(): got = lax.all_to_all(rows, ('gx', 'gy'), 0, 0, tiled=True)  12 us
    all_to_all x1, waiting for transfers between devices, shards(): got = lax.all_to_all(rows, ('gx', 'gy'), 0, 0, tiled=True)  9.32 us
    pallas_call x4, Pallas kernels, shards(): call(lambda *refs, rnd=rnd: middle_kernel(rnd, *refs), (sds(2, ROWS, 128)...  5.84 us
  transfers between devices with their start and end apart: 17, of which 12 were waited for; matrix products, arithmetic and copies ran while one was open for 0% of the time, Pallas kernels for 0%

profile of v1, /device:TPU:1, one launch (start us, length us, event | category | flops | bytes accessed | tf_op | source)
XLA Modules:
  0.0 96.0 jit_solution(17346193342154997572)
XLA Ops:
  1.3 1.1 %pack.1 = (f32[49,8,128]{2,1,0:T(8,128)S(1)}, f32[65,8,128]{2,1,0:T(8,128)S(1)}) custom-call(f32[3,8,8,128]{3,2,1,0:T(8,128)} %mix.1, f32[2,8,8,128]{3,2,1,0:T(8,128)} %forc.1, s32[8,8,128]{2,1,0:T(8,128)} %lab.1, f32[2,8,8,128]{3,2,1,0:T(8,128)} %basis.3, s32[8,128]{1,0:T(8,128)S(1)} %broadcast_in_dim.8.colour), custom_call_target="tpu_custom_call" | custom-call | tf_op jit(solution)/shard_map/pack/pallas_call | solution.py:423
  2.4 0.7 collective-permute-start
  3.0 9.6 %collective-permute-start.2 = (f32[49,8,128]{2,1,0:T(8,128)S(1)}, f32[49,8,128]{2,1,0:T(8,128)S(1)}, u32[]{:S(2)}, u32[]{:S(2)}) collective-permute-start(f32[49,8,128]{2,1,0:T(8,128)S(1)} %get-tuple-element.27), channel_id=1, source_target_pairs={{0,19},{1,0},{2,1},{3,2},{4,3},{5,16},{6,17},{7,18},{8,27},{9,8},{... | collective-permute-start | bytes 602120 | tf_op jit(solution)/shard_map/ppermute | solution.py:35
  12.6 3.4 %collective-permute-done.2.right = f32[49,8,128]{2,1,0:T(8,128)S(1)} collective-permute-done((f32[49,8,128]{2,1,0:T(8,128)S(1)}, f32[49,8,128]{2,1,0:T(8,128)S(1)}, u32[]{:S(2)}, u32[]{:S(2)}) %collective-permute-start.2) | collective-permute-done | bytes 200736 | tf_op jit(solution)/shard_map/ppermute | solution.py:35
  16.0 3.9 %collective-permute-done.1.left = f32[49,8,128]{2,1,0:T(8,128)S(1)} collective-permute-done((f32[49,8,128]{2,1,0:T(8,128)S(1)}, f32[49,8,128]{2,1,0:T(8,128)S(1)}, u32[]{:S(2)}, u32[]{:S(2)}) %collective-permute-start.1) | collective-permute-done | bytes 200736 | tf_op jit(solution)/shard_map/ppermute | solution.py:35
  20.1 2.2 %collective-permute-start.3 = (f32[27,8,384]{2,1,0:T(8,128)S(1)}, f32[27,8,384]{2,1,0:T(8,128)S(1)}, u32[]{:S(2)}, u32[]{:S(2)}) collective-permute-start(f32[27,8,384]{2,1,0:T(8,128)S(1)} %get-tuple-element.28), channel_id=1, source_target_pairs={{0,8},{1,9},{2,10},{3,11},{16,24},{17,25},{18,26},{19,27},{8,0},{9... | collective-permute-start | bytes 995336 | tf_op jit(solution)/shard_map/ppermute | solution.py:35
  22.3 7.5 %collective-permute-start.4 = (f32[27,8,384]{2,1,0:T(8,128)S(1)}, f32[27,8,384]{2,1,0:T(8,128)S(1)}, u32[]{:S(2)}, u32[]{:S(2)}) collective-permute-start(f32[27,8,384]{2,1,0:T(8,128)S(1)} %get-tuple-element.29), channel_id=1, source_target_pairs={{0,12},{1,13},{2,14},{3,15},{16,28},{17,29},{18,30},{19,31},{8,32}... | collective-permute-start | bytes 995336 | tf_op jit(solution)/shard_map/ppermute | solution.py:35
  29.8 4.8 %collective-permute-done.4.second = f32[27,8,384]{2,1,0:T(8,128)S(1)} collective-permute-done((f32[27,8,384]{2,1,0:T(8,128)S(1)}, f32[27,8,384]{2,1,0:T(8,128)S(1)}, u32[]{:S(2)}, u32[]{:S(2)}) %collective-permute-start.4) | collective-permute-done | bytes 331808 | tf_op jit(solution)/shard_map/ppermute | solution.py:35
  34.6 0.9 round0.1
  35.5 0.1 collective-permute-start.5
  35.6 7.7 %collective-permute-start.6 = (f32[224,128]{1,0:T(8,128)S(1)}, f32[224,128]{1,0:T(8,128)S(1)}, u32[]{:S(2)}, u32[]{:S(2)}) collective-permute-start(f32[224,128]{1,0:T(8,128)S(1)} %get-tuple-element.34), channel_id=1, source_target_pairs={{0,12},{1,13},{2,14},{3,15},{16,28},{17,29},{18,30},{19,31},{8,32}... | collective-permute-start | bytes 344072 | tf_op jit(solution)/shard_map/ppermute | solution.py:35
  43.3 2.5 %collective-permute-done.6.refs_4_ = f32[224,128]{1,0:T(8,128)S(1)} collective-permute-done((f32[224,128]{1,0:T(8,128)S(1)}, f32[224,128]{1,0:T(8,128)S(1)}, u32[]{:S(2)}, u32[]{:S(2)}) %collective-permute-start.6) | collective-permute-done | bytes 114720 | tf_op jit(solution)/shard_map/ppermute | solution.py:35
  45.7 3.7 %round1.1 = (f32[2,400,128]{2,1,0:T(8,128)S(1)}, f32[192,128]{1,0:T(8,128)S(1)}, f32[192,128]{1,0:T(8,128)S(1)}) custom-call(f32[5,400,128]{2,1,0:T(8,128)S(1)} %get-tuple-element.30.refs_0_.stat, f32[2,400,128]{2,1,0:T(8,128)S(1)} %get-tuple-element.31.refs_1_, f32[24,128]{1,0:T(8,128)S(1)} %get-tuple-element.32.refs_2_.meta, ...), custom_call_target="tpu_custom_call" | custom-call | tf_op jit(solution)/shard_map/round1/pallas_call | solution.py:451
  49.6 1.2 %collective-permute-done.7.refs_3_ = f32[192,128]{1,0:T(8,128)S(1)} collective-permute-done((f32[192,128]{1,0:T(8,128)S(1)}, f32[192,128]{1,0:T(8,128)S(1)}, u32[]{:S(2)}, u32[]{:S(2)}) %collective-permute-start.7) | collective-permute-done | bytes 98336 | tf_op jit(solution)/shard_map/ppermute | solution.py:35
  50.8 2.9 %collective-permute-done.8.refs_4_ = f32[192,128]{1,0:T(8,128)S(1)} collective-permute-done((f32[192,128]{1,0:T(8,128)S(1)}, f32[192,128]{1,0:T(8,128)S(1)}, u32[]{:S(2)}, u32[]{:S(2)}) %collective-permute-start.8) | collective-permute-done | bytes 98336 | tf_op jit(solution)/shard_map/ppermute | solution.py:35
  53.7 0.7 round2.1
  54.4 0.5 collective-permute-start.9
  54.9 0.9 collective-permute-done.9.refs_3_
  55.8 2.9 %collective-permute-done.10.refs_4_ = f32[160,128]{1,0:T(8,128)S(1)} collective-permute-done((f32[160,128]{1,0:T(8,128)S(1)}, f32[160,128]{1,0:T(8,128)S(1)}, u32[]{:S(2)}, u32[]{:S(2)}) %collective-permute-start.10) | collective-permute-done | bytes 81952 | tf_op jit(solution)/shard_map/ppermute | solution.py:35
  58.7 0.9 round3.1
  59.6 2.8 %collective-permute-start.11 = (f32[128,128]{1,0:T(8,128)S(1)}, f32[128,128]{1,0:T(8,128)S(1)}, u32[]{:S(2)}, u32[]{:S(2)}) collective-permute-start(f32[128,128]{1,0:T(8,128)S(1)} %get-tuple-element.42), channel_id=1, source_target_pairs={{0,8},{1,9},{2,10},{3,11},{16,24},{17,25},{18,26},{19,27},{8,0},{9... | collective-permute-start | bytes 196616 | tf_op jit(solution)/shard_map/ppermute | solution.py:35
  62.4 0.9 collective-permute-done.11.refs_3_
  63.3 2.8 %collective-permute-done.12.refs_4_ = f32[128,128]{1,0:T(8,128)S(1)} collective-permute-done((f32[128,128]{1,0:T(8,128)S(1)}, f32[128,128]{1,0:T(8,128)S(1)}, u32[]{:S(2)}, u32[]{:S(2)}) %collective-permute-start.12) | collective-permute-done | bytes 65568 | tf_op jit(solution)/shard_map/ppermute | solution.py:35
  66.1 0.6 round4.1
  66.7 0.2 collective-permute-start.13
  66.9 3.1 %collective-permute-start.14 = (f32[96,128]{1,0:T(8,128)S(1)}, f32[96,128]{1,0:T(8,128)S(1)}, u32[]{:S(2)}, u32[]{:S(2)}) collective-permute-start(f32[96,128]{1,0:T(8,128)S(1)} %get-tuple-element.46), channel_id=1, source_target_pairs={{0,12},{1,13},{2,14},{3,15},{16,28},{17,29},{18,30},{19,31},{8,32}... | collective-permute-start | bytes 147464 | tf_op jit(solution)/shard_map/ppermute | solution.py:35
  69.9 1.8 %collective-permute-done.14.second = f32[96,128]{1,0:T(8,128)S(1)} collective-permute-done((f32[96,128]{1,0:T(8,128)S(1)}, f32[96,128]{1,0:T(8,128)S(1)}, u32[]{:S(2)}, u32[]{:S(2)}) %collective-permute-start.14) | collective-permute-done | bytes 49184 | tf_op jit(solution)/shard_map/ppermute | solution.py:35
  71.7 1.4 %round5.1 = (f32[2,8,8,128]{3,2,1,0:T(8,128)S(1)}, f32[128,2,128]{2,1,0:T(2,128)}) custom-call(f32[5,400,128]{2,1,0:T(8,128)S(1)} %get-tuple-element.30.refs_0_.stat, f32[2,400,128]{2,1,0:T(8,128)S(1)} %get-tuple-element.44.u_in, f32[24,128]{1,0:T(8,128)S(1)} %get-tuple-element.32.refs_2_.meta, f32[96,128]{1,0:T(8,128)S(1)} %collective-permute-done.13.first, ...), custom_call_target="tpu_custom_call" | custom-call | tf_op jit(solution)/shard_map/round5/pallas_call | solution.py:458
  73.1 12.0 %all-to-all-start = ((f32[128,2,128]{2,1,0:T(2,128)}), f32[128,2,128]{2,1,0:T(2,128)S(1)}, u32[]{:S(2)}, u32[]{:S(2)}) async-start(f32[128,2,128]{2,1,0:T(2,128)} %get-tuple-element.48), calls=%async_computation | async-start | bytes 262144 | tf_op jit(solution)/shard_map/all_to_all | solution.py:465
  85.1 0.7 collective-permute-start.15
  85.8 9.3 %all-to-all-done.got = f32[128,2,128]{2,1,0:T(2,128)S(1)} async-done(((f32[128,2,128]{2,1,0:T(2,128)}), f32[128,2,128]{2,1,0:T(2,128)S(1)}, u32[]{:S(2)}, u32[]{:S(2)}) %all-to-all-start) | async-done | bytes 131104 | tf_op jit(solution)/shard_map/all_to_all | solution.py:465
  95.1 0.9 lift.1
  (16 shorter events, 0.3 us)
Async XLA Ops:
  2.4 17.6 %collective-permute-start = (f32[65,8,128]{2,1,0:T(8,128)S(1)}, f32[65,8,128]{2,1,0:T(8,128)S(1)}, u32[]{:S(2)}, u32[]{:S(2)}) collective-permute-start(f32[65,8,128]{2,1,0:T(8,128)S(1)} %get-tuple-element.26), channel_id=1, source_target_pairs={{0,0},{1,1},{2,2},{3,3},{4,16},{5,17},{6,18},{7,19},{8,8},{9,9},{1... | collective-permute-start | bytes 798728 | tf_op jit(solution)/shard_map/ppermute | solution.py:35
  3.0 13.0 %collective-permute-start.2 = (f32[49,8,128]{2,1,0:T(8,128)S(1)}, f32[49,8,128]{2,1,0:T(8,128)S(1)}, u32[]{:S(2)}, u32[]{:S(2)}) collective-permute-start(f32[49,8,128]{2,1,0:T(8,128)S(1)} %get-tuple-element.27), channel_id=1, source_target_pairs={{0,19},{1,0},{2,1},{3,2},{4,3},{5,16},{6,17},{7,18},{8,27},{9,8},{... | collective-permute-start | bytes 602120 | tf_op jit(solution)/shard_map/ppermute | solution.py:35
  12.6 7.4 %collective-permute-start.1 = (f32[49,8,128]{2,1,0:T(8,128)S(1)}, f32[49,8,128]{2,1,0:T(8,128)S(1)}, u32[]{:S(2)}, u32[]{:S(2)}) collective-permute-start(f32[49,8,128]{2,1,0:T(8,128)S(1)} %get-tuple-element.27), channel_id=1, source_target_pairs={{0,1},{1,2},{2,3},{3,16},{4,17},{5,18},{6,19},{7,0},{8,9},{9,10},{... | collective-permute-start | bytes 602120 | tf_op jit(solution)/shard_map/ppermute | solution.py:35
  20.1 9.7 %collective-permute-start.3 = (f32[27,8,384]{2,1,0:T(8,128)S(1)}, f32[27,8,384]{2,1,0:T(8,128)S(1)}, u32[]{:S(2)}, u32[]{:S(2)}) collective-permute-start(f32[27,8,384]{2,1,0:T(8,128)S(1)} %get-tuple-element.28), channel_id=1, source_target_pairs={{0,8},{1,9},{2,10},{3,11},{16,24},{17,25},{18,26},{19,27},{8,0},{9... | collective-permute-start | bytes 995336 | tf_op jit(solution)/shard_map/ppermute | solution.py:35
  22.3 12.3 %collective-permute-start.4 = (f32[27,8,384]{2,1,0:T(8,128)S(1)}, f32[27,8,384]{2,1,0:T(8,128)S(1)}, u32[]{:S(2)}, u32[]{:S(2)}) collective-permute-start(f32[27,8,384]{2,1,0:T(8,128)S(1)} %get-tuple-element.29), channel_id=1, source_target_pairs={{0,12},{1,13},{2,14},{3,15},{16,28},{17,29},{18,30},{19,31},{8,32}... | collective-permute-start | bytes 995336 | tf_op jit(solution)/shard_map/ppermute | solution.py:35
  35.5 7.8 %collective-permute-start.5 = (f32[224,128]{1,0:T(8,128)S(1)}, f32[224,128]{1,0:T(8,128)S(1)}, u32[]{:S(2)}, u32[]{:S(2)}) collective-permute-start(f32[224,128]{1,0:T(8,128)S(1)} %get-tuple-element.33), channel_id=1, source_target_pairs={{0,8},{1,9},{2,10},{3,11},{16,24},{17,25},{18,26},{19,27},{8,0},{9... | collective-permute-start | bytes 344072 | tf_op jit(solution)/shard_map/ppermute | solution.py:35
  35.6 10.2 %collective-permute-start.6 = (f32[224,128]{1,0:T(8,128)S(1)}, f32[224,128]{1,0:T(8,128)S(1)}, u32[]{:S(2)}, u32[]{:S(2)}) collective-permute-start(f32[224,128]{1,0:T(8,128)S(1)} %get-tuple-element.34), channel_id=1, source_target_pairs={{0,12},{1,13},{2,14},{3,15},{16,28},{17,29},{18,30},{19,31},{8,32}... | collective-permute-start | bytes 344072 | tf_op jit(solution)/shard_map/ppermute | solution.py:35
  49.4 1.4 %collective-permute-start.7 = (f32[192,128]{1,0:T(8,128)S(1)}, f32[192,128]{1,0:T(8,128)S(1)}, u32[]{:S(2)}, u32[]{:S(2)}) collective-permute-start(f32[192,128]{1,0:T(8,128)S(1)} %get-tuple-element.36), channel_id=1, source_target_pairs={{0,8},{1,9},{2,10},{3,11},{16,24},{17,25},{18,26},{19,27},{8,0},{9... | collective-permute-start | bytes 294920 | tf_op jit(solution)/shard_map/ppermute | solution.py:35
  49.5 4.1 %collective-permute-start.8 = (f32[192,128]{1,0:T(8,128)S(1)}, f32[192,128]{1,0:T(8,128)S(1)}, u32[]{:S(2)}, u32[]{:S(2)}) collective-permute-start(f32[192,128]{1,0:T(8,128)S(1)} %get-tuple-element.37), channel_id=1, source_target_pairs={{0,12},{1,13},{2,14},{3,15},{16,28},{17,29},{18,30},{19,31},{8,32}... | collective-permute-start | bytes 294920 | tf_op jit(solution)/shard_map/ppermute | solution.py:35
  54.4 1.4 %collective-permute-start.9 = (f32[160,128]{1,0:T(8,128)S(1)}, f32[160,128]{1,0:T(8,128)S(1)}, u32[]{:S(2)}, u32[]{:S(2)}) collective-permute-start(f32[160,128]{1,0:T(8,128)S(1)} %get-tuple-element.39), channel_id=1, source_target_pairs={{0,8},{1,9},{2,10},{3,11},{16,24},{17,25},{18,26},{19,27},{8,0},{9... | collective-permute-start | bytes 245768 | tf_op jit(solution)/shard_map/ppermute | solution.py:35
  54.9 3.9 %collective-permute-start.10 = (f32[160,128]{1,0:T(8,128)S(1)}, f32[160,128]{1,0:T(8,128)S(1)}, u32[]{:S(2)}, u32[]{:S(2)}) collective-permute-start(f32[160,128]{1,0:T(8,128)S(1)} %get-tuple-element.40), channel_id=1, source_target_pairs={{0,12},{1,13},{2,14},{3,15},{16,28},{17,29},{18,30},{19,31},{8,32}... | collective-permute-start | bytes 245768 | tf_op jit(solution)/shard_map/ppermute | solution.py:35
  59.6 3.7 %collective-permute-start.11 = (f32[128,128]{1,0:T(8,128)S(1)}, f32[128,128]{1,0:T(8,128)S(1)}, u32[]{:S(2)}, u32[]{:S(2)}) collective-permute-start(f32[128,128]{1,0:T(8,128)S(1)} %get-tuple-element.42), channel_id=1, source_target_pairs={{0,8},{1,9},{2,10},{3,11},{16,24},{17,25},{18,26},{19,27},{8,0},{9... | collective-permute-start | bytes 196616 | tf_op jit(solution)/shard_map/ppermute | solution.py:35
  62.4 3.7 %collective-permute-start.12 = (f32[128,128]{1,0:T(8,128)S(1)}, f32[128,128]{1,0:T(8,128)S(1)}, u32[]{:S(2)}, u32[]{:S(2)}) collective-permute-start(f32[128,128]{1,0:T(8,128)S(1)} %get-tuple-element.43), channel_id=1, source_target_pairs={{0,12},{1,13},{2,14},{3,15},{16,28},{17,29},{18,30},{19,31},{8,32}... | collective-permute-start | bytes 196616 | tf_op jit(solution)/shard_map/ppermute | solution.py:35
  66.7 3.2 %collective-permute-start.13 = (f32[96,128]{1,0:T(8,128)S(1)}, f32[96,128]{1,0:T(8,128)S(1)}, u32[]{:S(2)}, u32[]{:S(2)}) collective-permute-start(f32[96,128]{1,0:T(8,128)S(1)} %get-tuple-element.45), channel_id=1, source_target_pairs={{0,8},{1,9},{2,10},{3,11},{16,24},{17,25},{18,26},{19,27},{8,0},{9... | collective-permute-start | bytes 147464 | tf_op jit(solution)/shard_map/ppermute | solution.py:35
  66.9 4.8 %collective-permute-start.14 = (f32[96,128]{1,0:T(8,128)S(1)}, f32[96,128]{1,0:T(8,128)S(1)}, u32[]{:S(2)}, u32[]{:S(2)}) collective-permute-start(f32[96,128]{1,0:T(8,128)S(1)} %get-tuple-element.46), channel_id=1, source_target_pairs={{0,12},{1,13},{2,14},{3,15},{16,28},{17,29},{18,30},{19,31},{8,32}... | collective-permute-start | bytes 147464 | tf_op jit(solution)/shard_map/ppermute | solution.py:35
  73.1 22.0 %copy-start = (f32[2,8,8,128]{3,2,1,0:T(8,128)S(1)}, f32[2,8,8,128]{3,2,1,0:T(8,128)}, u32[]{:S(2)}) copy-start(f32[2,8,8,128]{3,2,1,0:T(8,128)} %basis.3) | copy-start | bytes 196612
  73.1 22.0 %copy-start.1 = (f32[1,1,2,256]{3,2,1,0:T(2,128)S(1)}, f32[1,1,2,256]{3,2,1,0:T(2,128)}, u32[]{:S(2)}) copy-start(f32[1,1,2,256]{3,2,1,0:T(2,128)} %inv.1) | copy-start | bytes 6148
  73.1 22.0 %all-to-all-start = ((f32[128,2,128]{2,1,0:T(2,128)}), f32[128,2,128]{2,1,0:T(2,128)S(1)}, u32[]{:S(2)}, u32[]{:S(2)}) async-start(f32[128,2,128]{2,1,0:T(2,128)} %get-tuple-element.48), calls=%async_computation | async-start | bytes 262144 | tf_op jit(solution)/shard_map/all_to_all | solution.py:465
  85.1 0.7 collective-permute-start.15

commit v2 on v1

--- a/solution.py
+++ b/solution.py
@@ -18,16 +18,16 @@
 
 
 def home(i, j):
-    pair, core = i // 2, i % 2
-    y, low = (pair, 0) if pair < 4 else (7 - pair, 1)
+    y, a, core = i // 4, i // 2 % 2, i % 2
+    low = a if y % 2 == 0 else 1 - a
     return (y * 4 + j // 4 * 2 + core) * NGY + low * 4 + j % 4
 
 
 def block_here():
     gx, gy = lax.axis_index("gx"), lax.axis_index("gy")
     y, low = gx // 4, gy // 4
-    pair = jnp.where(low == 0, y, 7 - y)
-    return pair * 2 + gx % 2, gx // 2 % 2 * 4 + gy % 4
+    a = jnp.where(y % 2 == 0, low, 1 - low)
+    return y * 4 + a * 2 + gx % 2, gx // 2 % 2 * 4 + gy % 4
 
 
 def send(x, to):
@@ -338,20 +338,22 @@
     emit(rnd, u, out1, out2, i % 2 == 0)
 
 
-def last_kernel(stat, u_in, meta, first, second, fin, own, nat, rows, u, uo, c0):
+def last_kernel(stat, u_in, meta, first, second, nat, u, uo, c0):
     i, j = block_here()
     u[...] = u_in[...]
     absorb(4, u, uo, first, second, i)
     solve_round(5, stat, u, uo, meta, (c0,), i, j)
+    for f in range(2):
+        flat = u[f, PAD + 128 : PAD + 256, :].T
+        for z in range(8):
+            nat[f, z] = flat[z * 16 + 4 : z * 16 + 12, :]
+
+
+def coarse_kernel(nat, own, fin, rows):
+    i, j = block_here()
     sub = iota((8, 128), 0)
     lane = iota((8, 128), 1)
-    tiles = []
-    for f in range(2):
-        flat = u[f, PAD + 128 : PAD + 256, :].T
-        for z in range(8):
-            tile = flat[z * 16 + 4 : z * 16 + 12, :]
-            nat[f, z] = tile
-            tiles.append(tile)
+    tiles = [nat[f, z] for f in range(2) for z in range(8)]
     cols = edge_columns(tiles)
     sums = [jnp.zeros((8, 128), F32) for _ in range(10)]
     left = cols * roll(fin[0], -16, 1)
@@ -455,15 +457,16 @@
             name=f"round{rnd}",
         )(stat, u, meta, one, two)
     one, two = swap(one, 0), swap(two, 1)
-    nat, rows = call(
+    nat = call(
         last_kernel,
-        (sds(2, 8, 8, 128), sds(NGX * NGY, 2, 128)),
+        sds(2, 8, 8, 128),
         [pltpu.VMEM((2, ROWS, 128), F32), pltpu.VMEM((2, ROWS, 128), F32), coef(17)],
         name="round5",
-    )(stat, u, meta, one, two, fin, own)
-    nat = send(nat, lambda i, j: (home(i, j), i * NGY + j))
+    )(stat, u, meta, one, two)
+    back = send(nat, lambda i, j: (home(i, j), i * NGY + j))
+    rows = call(coarse_kernel, sds(NGX * NGY, 2, 128), name="coarse")(nat, own, fin)
     got = lax.all_to_all(rows, ("gx", "gy"), 0, 0, tiled=True)
-    return call(lift_kernel, (sds(2, 8, 8, 128), sds(1, 1, 2)), name="lift")(got, coarse_inverse, coarse_basis, nat)
+    return call(lift_kernel, (sds(2, 8, 8, 128), sds(1, 1, 2)), name="lift")(got, coarse_inverse, coarse_basis, back)
 
 
 def solution(mesh):

time: 97.4 us -> 97.6 us (level); the launches traced: 96 us -> 99.2 us
  Pallas kernels: 10.1 us -> 12.7 us
    pallas_call x1, Pallas kernels: 0.85 us -> 3.58 us  [shards(): call(start_kernel, (sds(5, ROWS, 128), sds(2, ROWS, 128), sds(24, 128), s...]
    all_to_all x1, starting transfers between devices: 12 us -> 13.9 us  [shards(): got = lax.all_to_all(rows, ('gx', 'gy'), 0, 0, tiled=True)]
    ppermute x16, starting transfers between devices: 35.2 us -> 33.9 us  [send(): return lax.ppermute(x, ('gx', 'gy'), [to(i, j) for i, j in blocks])]
where the time goes in v2:
time: 97.6 us; the launch traced here: 99.2 us
  starting transfers between devices  47.8 us (49%)
  waiting for transfers between devices  37.4 us (38%)
  Pallas kernels  12.7 us (13%)
  between operations  1.4 us (1%)
    ppermute x16, starting transfers between devices, send(): return lax.ppermute(x, ('gx', 'gy'), [to(i, j) for i, j in blocks])  33.9 us
    ppermute x16, waiting for transfers between devices, send(): return lax.ppermute(x, ('gx', 'gy'), [to(i, j) for i, j in blocks])  28.1 us
    all_to_all x1, starting transfers between devices, shards(): got = lax.all_to_all(rows, ('gx', 'gy'), 0, 0, tiled=True)  13.9 us
    all_to_all x1, waiting for transfers between devices, shards(): got = lax.all_to_all(rows, ('gx', 'gy'), 0, 0, tiled=True)  9.32 us
    pallas_call x4, Pallas kernels, shards(): call(lambda *refs, rnd=rnd: middle_kernel(rnd, *refs), (sds(2, ROWS, 128)...  5.67 us
    pallas_call x1, Pallas kernels, shards(): call(start_kernel, (sds(5, ROWS, 128), sds(2, ROWS, 128), sds(24, 128), s...  3.58 us
  transfers between devices with their start and end apart: 17, of which 12 were waited for; matrix products, arithmetic and copies ran while one was open for 0% of the time, Pallas kernels for 0%

profile of v2, /device:TPU:1, one launch (start us, length us, event | category | flops | bytes accessed | tf_op | source)
XLA Modules:
  0.0 99.2 jit_solution(8724261888467037743)
XLA Ops:
  1.3 1.1 %pack.1 = (f32[49,8,128]{2,1,0:T(8,128)S(1)}, f32[65,8,128]{2,1,0:T(8,128)S(1)}) custom-call(f32[3,8,8,128]{3,2,1,0:T(8,128)} %mix.1, f32[2,8,8,128]{3,2,1,0:T(8,128)} %forc.1, s32[8,8,128]{2,1,0:T(8,128)} %lab.1, f32[2,8,8,128]{3,2,1,0:T(8,128)} %basis.3, s32[8,128]{1,0:T(8,128)S(1)} %broadcast_in_dim.8.colour), custom_call_target="tpu_custom_call" | custom-call | tf_op jit(solution)/shard_map/pack/pallas_call | solution.py:425
  2.4 0.7 collective-permute-start
  3.0 8.6 %collective-permute-start.2 = (f32[49,8,128]{2,1,0:T(8,128)S(1)}, f32[49,8,128]{2,1,0:T(8,128)S(1)}, u32[]{:S(2)}, u32[]{:S(2)}) collective-permute-start(f32[49,8,128]{2,1,0:T(8,128)S(1)} %get-tuple-element.25), channel_id=1, source_target_pairs={{0,19},{1,0},{2,1},{3,2},{4,3},{5,16},{6,17},{7,18},{8,27},{9,8},{... | collective-permute-start | bytes 602120 | tf_op jit(solution)/shard_map/ppermute | solution.py:35
  11.6 3.4 %collective-permute-done.2.right = f32[49,8,128]{2,1,0:T(8,128)S(1)} collective-permute-done((f32[49,8,128]{2,1,0:T(8,128)S(1)}, f32[49,8,128]{2,1,0:T(8,128)S(1)}, u32[]{:S(2)}, u32[]{:S(2)}) %collective-permute-start.2) | collective-permute-done | bytes 200736 | tf_op jit(solution)/shard_map/ppermute | solution.py:35
  15.1 3.9 %collective-permute-done.1.left = f32[49,8,128]{2,1,0:T(8,128)S(1)} collective-permute-done((f32[49,8,128]{2,1,0:T(8,128)S(1)}, f32[49,8,128]{2,1,0:T(8,128)S(1)}, u32[]{:S(2)}, u32[]{:S(2)}) %collective-permute-start.1) | collective-permute-done | bytes 200736 | tf_op jit(solution)/shard_map/ppermute | solution.py:35
  19.1 2.2 %collective-permute-start.3 = (f32[27,8,384]{2,1,0:T(8,128)S(1)}, f32[27,8,384]{2,1,0:T(8,128)S(1)}, u32[]{:S(2)}, u32[]{:S(2)}) collective-permute-start(f32[27,8,384]{2,1,0:T(8,128)S(1)} %get-tuple-element.26), channel_id=1, source_target_pairs={{0,8},{1,9},{2,10},{3,11},{16,24},{17,25},{18,26},{19,27},{8,0},{9... | collective-permute-start | bytes 995336 | tf_op jit(solution)/shard_map/ppermute | solution.py:35
  21.3 1.5 %collective-permute-start.4 = (f32[27,8,384]{2,1,0:T(8,128)S(1)}, f32[27,8,384]{2,1,0:T(8,128)S(1)}, u32[]{:S(2)}, u32[]{:S(2)}) collective-permute-start(f32[27,8,384]{2,1,0:T(8,128)S(1)} %get-tuple-element.27), channel_id=1, source_target_pairs={{0,104},{1,105},{2,106},{3,107},{16,120},{17,121},{18,122},{19,123... | collective-permute-start | bytes 995336 | tf_op jit(solution)/shard_map/ppermute | solution.py:35
  22.9 5.0 %collective-permute-done.4.second = f32[27,8,384]{2,1,0:T(8,128)S(1)} collective-permute-done((f32[27,8,384]{2,1,0:T(8,128)S(1)}, f32[27,8,384]{2,1,0:T(8,128)S(1)}, u32[]{:S(2)}, u32[]{:S(2)}) %collective-permute-start.4) | collective-permute-done | bytes 331808 | tf_op jit(solution)/shard_map/ppermute | solution.py:35
  27.9 3.6 %round0.1 = (f32[5,400,128]{2,1,0:T(8,128)S(1)}, f32[2,400,128]{2,1,0:T(8,128)S(1)}, f32[24,128]{1,0:T(8,128)S(1)}, f32[6,8,128]{2,1,0:T(8,128)S(1)}, f32[224,128]{1,0:T(8,128)S(1)}, /*index=5*/f32[224,128]{1,0:T(8,128)S(1)}) custom-call(f32[65,8,128]{2,1,0:T(8,128)S(1)} %collective-permute-done.own, f32[49,8,128]{2,1,0:T(8,128)S(1)} %collective-permute-done.1.left, ...), custom_call_target="tpu_custom_call" | custom-call | tf_op jit(solution)/shard_map/round0/pallas_call | solution.py:444
  31.4 5.0 %collective-permute-start.5 = (f32[224,128]{1,0:T(8,128)S(1)}, f32[224,128]{1,0:T(8,128)S(1)}, u32[]{:S(2)}, u32[]{:S(2)}) collective-permute-start(f32[224,128]{1,0:T(8,128)S(1)} %get-tuple-element.31), channel_id=1, source_target_pairs={{0,8},{1,9},{2,10},{3,11},{16,24},{17,25},{18,26},{19,27},{8,0},{9... | collective-permute-start | bytes 344072 | tf_op jit(solution)/shard_map/ppermute | solution.py:35
  36.5 1.0 collective-permute-done.5.refs_3_
  37.5 3.5 %collective-permute-done.6.refs_4_ = f32[224,128]{1,0:T(8,128)S(1)} collective-permute-done((f32[224,128]{1,0:T(8,128)S(1)}, f32[224,128]{1,0:T(8,128)S(1)}, u32[]{:S(2)}, u32[]{:S(2)}) %collective-permute-start.6) | collective-permute-done | bytes 114720 | tf_op jit(solution)/shard_map/ppermute | solution.py:35
  41.0 1.0 round1.1
  42.0 1.1 %collective-permute-start.7 = (f32[192,128]{1,0:T(8,128)S(1)}, f32[192,128]{1,0:T(8,128)S(1)}, u32[]{:S(2)}, u32[]{:S(2)}) collective-permute-start(f32[192,128]{1,0:T(8,128)S(1)} %get-tuple-element.34), channel_id=1, source_target_pairs={{0,8},{1,9},{2,10},{3,11},{16,24},{17,25},{18,26},{19,27},{8,0},{9... | collective-permute-start | bytes 294920 | tf_op jit(solution)/shard_map/ppermute | solution.py:35
  43.1 5.6 %collective-permute-start.8 = (f32[192,128]{1,0:T(8,128)S(1)}, f32[192,128]{1,0:T(8,128)S(1)}, u32[]{:S(2)}, u32[]{:S(2)}) collective-permute-start(f32[192,128]{1,0:T(8,128)S(1)} %get-tuple-element.35), channel_id=1, source_target_pairs={{0,104},{1,105},{2,106},{3,107},{16,120},{17,121},{18,122},{19,123... | collective-permute-start | bytes 294920 | tf_op jit(solution)/shard_map/ppermute | solution.py:35
  48.7 2.3 %collective-permute-done.8.refs_4_ = f32[192,128]{1,0:T(8,128)S(1)} collective-permute-done((f32[192,128]{1,0:T(8,128)S(1)}, f32[192,128]{1,0:T(8,128)S(1)}, u32[]{:S(2)}, u32[]{:S(2)}) %collective-permute-start.8) | collective-permute-done | bytes 98336 | tf_op jit(solution)/shard_map/ppermute | solution.py:35
  51.0 0.7 round2.1
  51.8 1.8 %collective-permute-start.10 = (f32[160,128]{1,0:T(8,128)S(1)}, f32[160,128]{1,0:T(8,128)S(1)}, u32[]{:S(2)}, u32[]{:S(2)}) collective-permute-start(f32[160,128]{1,0:T(8,128)S(1)} %get-tuple-element.38), channel_id=1, source_target_pairs={{0,104},{1,105},{2,106},{3,107},{16,120},{17,121},{18,122},{19,123... | collective-permute-start | bytes 245768 | tf_op jit(solution)/shard_map/ppermute | solution.py:35
  53.7 2.1 %collective-permute-done.10.refs_4_ = f32[160,128]{1,0:T(8,128)S(1)} collective-permute-done((f32[160,128]{1,0:T(8,128)S(1)}, f32[160,128]{1,0:T(8,128)S(1)}, u32[]{:S(2)}, u32[]{:S(2)}) %collective-permute-start.10) | collective-permute-done | bytes 81952 | tf_op jit(solution)/shard_map/ppermute | solution.py:35
  55.8 0.9 round3.1
  56.7 4.4 %collective-permute-start.11 = (f32[128,128]{1,0:T(8,128)S(1)}, f32[128,128]{1,0:T(8,128)S(1)}, u32[]{:S(2)}, u32[]{:S(2)}) collective-permute-start(f32[128,128]{1,0:T(8,128)S(1)} %get-tuple-element.40), channel_id=1, source_target_pairs={{0,8},{1,9},{2,10},{3,11},{16,24},{17,25},{18,26},{19,27},{8,0},{9... | collective-permute-start | bytes 196616 | tf_op jit(solution)/shard_map/ppermute | solution.py:35
  61.5 0.5 collective-permute-done.11.refs_3_
  62.0 2.8 %collective-permute-done.12.refs_4_ = f32[128,128]{1,0:T(8,128)S(1)} collective-permute-done((f32[128,128]{1,0:T(8,128)S(1)}, f32[128,128]{1,0:T(8,128)S(1)}, u32[]{:S(2)}, u32[]{:S(2)}) %collective-permute-start.12) | collective-permute-done | bytes 65568 | tf_op jit(solution)/shard_map/ppermute | solution.py:35
  64.8 3.1 %round4.1 = (f32[2,400,128]{2,1,0:T(8,128)S(1)}, f32[96,128]{1,0:T(8,128)S(1)}, f32[96,128]{1,0:T(8,128)S(1)}) custom-call(f32[5,400,128]{2,1,0:T(8,128)S(1)} %get-tuple-element.28.refs_0_.stat, f32[2,400,128]{2,1,0:T(8,128)S(1)} %get-tuple-element.39.refs_1_, f32[24,128]{1,0:T(8,128)S(1)} %get-tuple-element.30.refs_2_.meta, ...), custom_call_target="tpu_custom_call" | custom-call | tf_op jit(solution)/shard_map/round4/pallas_call | solution.py:453
  67.9 1.6 %collective-permute-start.13 = (f32[96,128]{1,0:T(8,128)S(1)}, f32[96,128]{1,0:T(8,128)S(1)}, u32[]{:S(2)}, u32[]{:S(2)}) collective-permute-start(f32[96,128]{1,0:T(8,128)S(1)} %get-tuple-element.43), channel_id=1, source_target_pairs={{0,8},{1,9},{2,10},{3,11},{16,24},{17,25},{18,26},{19,27},{8,0},{9... | collective-permute-start | bytes 147464 | tf_op jit(solution)/shard_map/ppermute | solution.py:35
  69.5 0.9 collective-permute-done.13.first
  70.4 2.6 %collective-permute-done.14.second = f32[96,128]{1,0:T(8,128)S(1)} collective-permute-done((f32[96,128]{1,0:T(8,128)S(1)}, f32[96,128]{1,0:T(8,128)S(1)}, u32[]{:S(2)}, u32[]{:S(2)}) %collective-permute-start.14) | collective-permute-done | bytes 49184 | tf_op jit(solution)/shard_map/ppermute | solution.py:35
  73.5 0.9 coarse.1
  74.5 13.9 %all-to-all-start = ((f32[128,2,128]{2,1,0:T(2,128)}), f32[128,2,128]{2,1,0:T(2,128)S(1)}, u32[]{:S(2)}, u32[]{:S(2)}) async-start(f32[128,2,128]{2,1,0:T(2,128)} %coarse.1), calls=%async_computation | async-start | bytes 262144 | tf_op jit(solution)/shard_map/all_to_all | solution.py:468
  88.3 0.7 collective-permute-start.15
  89.0 9.3 %all-to-all-done.got = f32[128,2,128]{2,1,0:T(2,128)S(1)} async-done(((f32[128,2,128]{2,1,0:T(2,128)}), f32[128,2,128]{2,1,0:T(2,128)S(1)}, u32[]{:S(2)}, u32[]{:S(2)}) %all-to-all-start) | async-done | bytes 131104 | tf_op jit(solution)/shard_map/all_to_all | solution.py:468
  98.3 0.9 lift.1
  (17 shorter events, 1.1 us)
Async XLA Ops:
  2.4 16.6 %collective-permute-start = (f32[65,8,128]{2,1,0:T(8,128)S(1)}, f32[65,8,128]{2,1,0:T(8,128)S(1)}, u32[]{:S(2)}, u32[]{:S(2)}) collective-permute-start(f32[65,8,128]{2,1,0:T(8,128)S(1)} %get-tuple-element.24), channel_id=1, source_target_pairs={{0,0},{1,1},{2,2},{3,3},{4,16},{5,17},{6,18},{7,19},{8,8},{9,9},{1... | collective-permute-start | bytes 798728 | tf_op jit(solution)/shard_map/ppermute | solution.py:35
  3.0 12.0 %collective-permute-start.2 = (f32[49,8,128]{2,1,0:T(8,128)S(1)}, f32[49,8,128]{2,1,0:T(8,128)S(1)}, u32[]{:S(2)}, u32[]{:S(2)}) collective-permute-start(f32[49,8,128]{2,1,0:T(8,128)S(1)} %get-tuple-element.25), channel_id=1, source_target_pairs={{0,19},{1,0},{2,1},{3,2},{4,3},{5,16},{6,17},{7,18},{8,27},{9,8},{... | collective-permute-start | bytes 602120 | tf_op jit(solution)/shard_map/ppermute | solution.py:35
  11.6 7.4 %collective-permute-start.1 = (f32[49,8,128]{2,1,0:T(8,128)S(1)}, f32[49,8,128]{2,1,0:T(8,128)S(1)}, u32[]{:S(2)}, u32[]{:S(2)}) collective-permute-start(f32[49,8,128]{2,1,0:T(8,128)S(1)} %get-tuple-element.25), channel_id=1, source_target_pairs={{0,1},{1,2},{2,3},{3,16},{4,17},{5,18},{6,19},{7,0},{8,9},{9,10},{... | collective-permute-start | bytes 602120 | tf_op jit(solution)/shard_map/ppermute | solution.py:35
  19.1 3.8 %collective-permute-start.3 = (f32[27,8,384]{2,1,0:T(8,128)S(1)}, f32[27,8,384]{2,1,0:T(8,128)S(1)}, u32[]{:S(2)}, u32[]{:S(2)}) collective-permute-start(f32[27,8,384]{2,1,0:T(8,128)S(1)} %get-tuple-element.26), channel_id=1, source_target_pairs={{0,8},{1,9},{2,10},{3,11},{16,24},{17,25},{18,26},{19,27},{8,0},{9... | collective-permute-start | bytes 995336 | tf_op jit(solution)/shard_map/ppermute | solution.py:35
  21.3 6.5 %collective-permute-start.4 = (f32[27,8,384]{2,1,0:T(8,128)S(1)}, f32[27,8,384]{2,1,0:T(8,128)S(1)}, u32[]{:S(2)}, u32[]{:S(2)}) collective-permute-start(f32[27,8,384]{2,1,0:T(8,128)S(1)} %get-tuple-element.27), channel_id=1, source_target_pairs={{0,104},{1,105},{2,106},{3,107},{16,120},{17,121},{18,122},{19,123... | collective-permute-start | bytes 995336 | tf_op jit(solution)/shard_map/ppermute | solution.py:35
  31.4 6.0 %collective-permute-start.5 = (f32[224,128]{1,0:T(8,128)S(1)}, f32[224,128]{1,0:T(8,128)S(1)}, u32[]{:S(2)}, u32[]{:S(2)}) collective-permute-start(f32[224,128]{1,0:T(8,128)S(1)} %get-tuple-element.31), channel_id=1, source_target_pairs={{0,8},{1,9},{2,10},{3,11},{16,24},{17,25},{18,26},{19,27},{8,0},{9... | collective-permute-start | bytes 344072 | tf_op jit(solution)/shard_map/ppermute | solution.py:35
  36.5 4.5 %collective-permute-start.6 = (f32[224,128]{1,0:T(8,128)S(1)}, f32[224,128]{1,0:T(8,128)S(1)}, u32[]{:S(2)}, u32[]{:S(2)}) collective-permute-start(f32[224,128]{1,0:T(8,128)S(1)} %get-tuple-element.32), channel_id=1, source_target_pairs={{0,104},{1,105},{2,106},{3,107},{16,120},{17,121},{18,122},{19,123... | collective-permute-start | bytes 344072 | tf_op jit(solution)/shard_map/ppermute | solution.py:35
  42.0 6.7 %collective-permute-start.7 = (f32[192,128]{1,0:T(8,128)S(1)}, f32[192,128]{1,0:T(8,128)S(1)}, u32[]{:S(2)}, u32[]{:S(2)}) collective-permute-start(f32[192,128]{1,0:T(8,128)S(1)} %get-tuple-element.34), channel_id=1, source_target_pairs={{0,8},{1,9},{2,10},{3,11},{16,24},{17,25},{18,26},{19,27},{8,0},{9... | collective-permute-start | bytes 294920 | tf_op jit(solution)/shard_map/ppermute | solution.py:35
  43.1 7.9 %collective-permute-start.8 = (f32[192,128]{1,0:T(8,128)S(1)}, f32[192,128]{1,0:T(8,128)S(1)}, u32[]{:S(2)}, u32[]{:S(2)}) collective-permute-start(f32[192,128]{1,0:T(8,128)S(1)} %get-tuple-element.35), channel_id=1, source_target_pairs={{0,104},{1,105},{2,106},{3,107},{16,120},{17,121},{18,122},{19,123... | collective-permute-start | bytes 294920 | tf_op jit(solution)/shard_map/ppermute | solution.py:35
  51.7 1.9 %collective-permute-start.9 = (f32[160,128]{1,0:T(8,128)S(1)}, f32[160,128]{1,0:T(8,128)S(1)}, u32[]{:S(2)}, u32[]{:S(2)}) collective-permute-start(f32[160,128]{1,0:T(8,128)S(1)} %get-tuple-element.37), channel_id=1, source_target_pairs={{0,8},{1,9},{2,10},{3,11},{16,24},{17,25},{18,26},{19,27},{8,0},{9... | collective-permute-start | bytes 245768 | tf_op jit(solution)/shard_map/ppermute | solution.py:35
  51.8 4.0 %collective-permute-start.10 = (f32[160,128]{1,0:T(8,128)S(1)}, f32[160,128]{1,0:T(8,128)S(1)}, u32[]{:S(2)}, u32[]{:S(2)}) collective-permute-start(f32[160,128]{1,0:T(8,128)S(1)} %get-tuple-element.38), channel_id=1, source_target_pairs={{0,104},{1,105},{2,106},{3,107},{16,120},{17,121},{18,122},{19,123... | collective-permute-start | bytes 245768 | tf_op jit(solution)/shard_map/ppermute | solution.py:35
  56.7 5.3 %collective-permute-start.11 = (f32[128,128]{1,0:T(8,128)S(1)}, f32[128,128]{1,0:T(8,128)S(1)}, u32[]{:S(2)}, u32[]{:S(2)}) collective-permute-start(f32[128,128]{1,0:T(8,128)S(1)} %get-tuple-element.40), channel_id=1, source_target_pairs={{0,8},{1,9},{2,10},{3,11},{16,24},{17,25},{18,26},{19,27},{8,0},{9... | collective-permute-start | bytes 196616 | tf_op jit(solution)/shard_map/ppermute | solution.py:35
  61.1 3.7 %collective-permute-start.12 = (f32[128,128]{1,0:T(8,128)S(1)}, f32[128,128]{1,0:T(8,128)S(1)}, u32[]{:S(2)}, u32[]{:S(2)}) collective-permute-start(f32[128,128]{1,0:T(8,128)S(1)} %get-tuple-element.41), channel_id=1, source_target_pairs={{0,104},{1,105},{2,106},{3,107},{16,120},{17,121},{18,122},{19,123... | collective-permute-start | bytes 196616 | tf_op jit(solution)/shard_map/ppermute | solution.py:35
  67.9 2.5 %collective-permute-start.13 = (f32[96,128]{1,0:T(8,128)S(1)}, f32[96,128]{1,0:T(8,128)S(1)}, u32[]{:S(2)}, u32[]{:S(2)}) collective-permute-start(f32[96,128]{1,0:T(8,128)S(1)} %get-tuple-element.43), channel_id=1, source_target_pairs={{0,8},{1,9},{2,10},{3,11},{16,24},{17,25},{18,26},{19,27},{8,0},{9... | collective-permute-start | bytes 147464 | tf_op jit(solution)/shard_map/ppermute | solution.py:35
  69.5 3.5 %collective-permute-start.14 = (f32[96,128]{1,0:T(8,128)S(1)}, f32[96,128]{1,0:T(8,128)S(1)}, u32[]{:S(2)}, u32[]{:S(2)}) collective-permute-start(f32[96,128]{1,0:T(8,128)S(1)} %get-tuple-element.44), channel_id=1, source_target_pairs={{0,104},{1,105},{2,106},{3,107},{16,120},{17,121},{18,122},{19,123... | collective-permute-start | bytes 147464 | tf_op jit(solution)/shard_map/ppermute | solution.py:35
  74.4 23.9 %copy-start = (f32[2,8,8,128]{3,2,1,0:T(8,128)S(1)}, f32[2,8,8,128]{3,2,1,0:T(8,128)}, u32[]{:S(2)}) copy-start(f32[2,8,8,128]{3,2,1,0:T(8,128)} %basis.3) | copy-start | bytes 196612
  74.5 23.9 %copy-start.1 = (f32[1,1,2,256]{3,2,1,0:T(2,128)S(1)}, f32[1,1,2,256]{3,2,1,0:T(2,128)}, u32[]{:S(2)}) copy-start(f32[1,1,2,256]{3,2,1,0:T(2,128)} %inv.1) | copy-start | bytes 6148
  74.5 23.9 %all-to-all-start = ((f32[128,2,128]{2,1,0:T(2,128)}), f32[128,2,128]{2,1,0:T(2,128)S(1)}, u32[]{:S(2)}, u32[]{:S(2)}) async-start(f32[128,2,128]{2,1,0:T(2,128)} %coarse.1), calls=%async_computation | async-start | bytes 262144 | tf_op jit(solution)/shard_map/all_to_all | solution.py:468
  88.3 0.7 collective-permute-start.15

commit v3 on v2

--- a/solution.py
+++ b/solution.py
@@ -7,7 +7,7 @@
 
 SWEEPS = 20
 OMEGA = 0.8
-UNROLL = 19
+UNROLL = 6
 PAD = 8
 WIN = (16, 13, 10, 7, 4)
 KEEP = (104, 80, 56, 32, 8)
@@ -347,6 +347,8 @@
         flat = u[f, PAD + 128 : PAD + 256, :].T
         for z in range(8):
             nat[f, z] = flat[z * 16 + 4 : z * 16 + 12, :]
+    for f in range(2, nat.shape[0]):
+        nat[f] = jnp.zeros((8, 8, 128), F32)
 
 
 def coarse_kernel(nat, own, fin, rows):
@@ -459,7 +461,7 @@
     one, two = swap(one, 0), swap(two, 1)
     nat = call(
         last_kernel,
-        sds(2, 8, 8, 128),
+        sds(4, 8, 8, 128),
         [pltpu.VMEM((2, ROWS, 128), F32), pltpu.VMEM((2, ROWS, 128), F32), coef(17)],
         name="round5",
     )(stat, u, meta, one, two)

time: 97.6 us -> 100 us (1.025); the launches traced: 99.2 us -> 99.3 us
  blocking collectives: 0 us -> 23.7 us
  starting transfers between devices: 47.8 us -> 32.8 us
  waiting for transfers between devices: 37.4 us -> 29.1 us
    all_to_all x0 -> x1, blocking collectives: none -> 23.7 us  [shards(): got = lax.all_to_all(rows, ('gx', 'gy'), 0, 0, tiled=True)]
    all_to_all x1 -> x0, starting transfers between devices: 13.9 us -> none  [shards(): got = lax.all_to_all(rows, ('gx', 'gy'), 0, 0, tiled=True)]
    all_to_all x1 -> x0, waiting for transfers between devices: 9.32 us -> none  [shards(): got = lax.all_to_all(rows, ('gx', 'gy'), 0, 0, tiled=True)]
    ppermute x16, starting transfers between devices: 33.9 us -> 32.8 us  [send(): return lax.ppermute(x, ('gx', 'gy'), [to(i, j) for i, j in blocks])]
    ppermute x16, waiting for transfers between devices: 28.1 us -> 29.1 us  [send(): return lax.ppermute(x, ('gx', 'gy'), [to(i, j) for i, j in blocks])]
  transfers between devices with their start and end apart: 17 -> 16, of which waited for: 12 -> 11; matrix products, arithmetic and copies ran while one was open for 0% -> 0% of each run, Pallas kernels for 0% -> 0%
where the time goes in v3:
time: 100 us; the launch traced here: 99.3 us
  starting transfers between devices  32.8 us (33%)
  waiting for transfers between devices  29.1 us (29%)
  blocking collectives  23.7 us (24%)
  Pallas kernels  12.3 us (12%)
  between operations  1.41 us (1%)
    ppermute x16, starting transfers between devices, send(): return lax.ppermute(x, ('gx', 'gy'), [to(i, j) for i, j in blocks])  32.8 us
    ppermute x16, waiting for transfers between devices, send(): return lax.ppermute(x, ('gx', 'gy'), [to(i, j) for i, j in blocks])  29.1 us
    all_to_all x1, blocking collectives, shards(): got = lax.all_to_all(rows, ('gx', 'gy'), 0, 0, tiled=True)  23.7 us
    pallas_call x4, Pallas kernels, shards(): call(lambda *refs, rnd=rnd: middle_kernel(rnd, *refs), (sds(2, ROWS, 128)...  5.63 us
    pallas_call x1, Pallas kernels, shards(): call(start_kernel, (sds(5, ROWS, 128), sds(2, ROWS, 128), sds(24, 128), s...  3.86 us
  transfers between devices with their start and end apart: 16, of which 11 were waited for; matrix products, arithmetic and copies ran while one was open for 0% of the time, Pallas kernels for 0%

profile of v3, /device:TPU:1, one launch (start us, length us, event | category | flops | bytes accessed | tf_op | source)
XLA Modules:
  0.0 99.3 jit_solution(11935464266282315040)
XLA Ops:
  1.3 1.1 %pack.1 = (f32[49,8,128]{2,1,0:T(8,128)S(1)}, f32[65,8,128]{2,1,0:T(8,128)S(1)}) custom-call(f32[3,8,8,128]{3,2,1,0:T(8,128)} %mix.1, f32[2,8,8,128]{3,2,1,0:T(8,128)} %forc.1, s32[8,8,128]{2,1,0:T(8,128)} %lab.1, f32[2,8,8,128]{3,2,1,0:T(8,128)} %basis.3, s32[8,128]{1,0:T(8,128)S(1)} %broadcast_in_dim.8.colour), custom_call_target="tpu_custom_call" | custom-call | tf_op jit(solution)/shard_map/pack/pallas_call | solution.py:427
  2.4 0.7 collective-permute-start
  3.0 8.6 %collective-permute-start.2 = (f32[49,8,128]{2,1,0:T(8,128)S(1)}, f32[49,8,128]{2,1,0:T(8,128)S(1)}, u32[]{:S(2)}, u32[]{:S(2)}) collective-permute-start(f32[49,8,128]{2,1,0:T(8,128)S(1)} %get-tuple-element.25), channel_id=1, source_target_pairs={{0,19},{1,0},{2,1},{3,2},{4,3},{5,16},{6,17},{7,18},{8,27},{9,8},{... | collective-permute-start | bytes 602120 | tf_op jit(solution)/shard_map/ppermute | solution.py:35
  11.6 3.4 %collective-permute-done.2.right = f32[49,8,128]{2,1,0:T(8,128)S(1)} collective-permute-done((f32[49,8,128]{2,1,0:T(8,128)S(1)}, f32[49,8,128]{2,1,0:T(8,128)S(1)}, u32[]{:S(2)}, u32[]{:S(2)}) %collective-permute-start.2) | collective-permute-done | bytes 200736 | tf_op jit(solution)/shard_map/ppermute | solution.py:35
  15.1 3.9 %collective-permute-done.1.left = f32[49,8,128]{2,1,0:T(8,128)S(1)} collective-permute-done((f32[49,8,128]{2,1,0:T(8,128)S(1)}, f32[49,8,128]{2,1,0:T(8,128)S(1)}, u32[]{:S(2)}, u32[]{:S(2)}) %collective-permute-start.1) | collective-permute-done | bytes 200736 | tf_op jit(solution)/shard_map/ppermute | solution.py:35
  19.1 2.2 %collective-permute-start.3 = (f32[27,8,384]{2,1,0:T(8,128)S(1)}, f32[27,8,384]{2,1,0:T(8,128)S(1)}, u32[]{:S(2)}, u32[]{:S(2)}) collective-permute-start(f32[27,8,384]{2,1,0:T(8,128)S(1)} %get-tuple-element.26), channel_id=1, source_target_pairs={{0,8},{1,9},{2,10},{3,11},{16,24},{17,25},{18,26},{19,27},{8,0},{9... | collective-permute-start | bytes 995336 | tf_op jit(solution)/shard_map/ppermute | solution.py:35
  21.3 1.5 %collective-permute-start.4 = (f32[27,8,384]{2,1,0:T(8,128)S(1)}, f32[27,8,384]{2,1,0:T(8,128)S(1)}, u32[]{:S(2)}, u32[]{:S(2)}) collective-permute-start(f32[27,8,384]{2,1,0:T(8,128)S(1)} %get-tuple-element.27), channel_id=1, source_target_pairs={{0,104},{1,105},{2,106},{3,107},{16,120},{17,121},{18,122},{19,123... | collective-permute-start | bytes 995336 | tf_op jit(solution)/shard_map/ppermute | solution.py:35
  22.9 5.0 %collective-permute-done.4.second = f32[27,8,384]{2,1,0:T(8,128)S(1)} collective-permute-done((f32[27,8,384]{2,1,0:T(8,128)S(1)}, f32[27,8,384]{2,1,0:T(8,128)S(1)}, u32[]{:S(2)}, u32[]{:S(2)}) %collective-permute-start.4) | collective-permute-done | bytes 331808 | tf_op jit(solution)/shard_map/ppermute | solution.py:35
  27.9 3.9 %round0.1 = (f32[5,400,128]{2,1,0:T(8,128)S(1)}, f32[2,400,128]{2,1,0:T(8,128)S(1)}, f32[24,128]{1,0:T(8,128)S(1)}, f32[6,8,128]{2,1,0:T(8,128)S(1)}, f32[224,128]{1,0:T(8,128)S(1)}, /*index=5*/f32[224,128]{1,0:T(8,128)S(1)}) custom-call(f32[65,8,128]{2,1,0:T(8,128)S(1)} %collective-permute-done.own, f32[49,8,128]{2,1,0:T(8,128)S(1)} %collective-permute-done.1.left, ...), custom_call_target="tpu_custom_call" | custom-call | tf_op jit(solution)/shard_map/round0/pallas_call | solution.py:446
  31.7 7.8 %collective-permute-start.5 = (f32[224,128]{1,0:T(8,128)S(1)}, f32[224,128]{1,0:T(8,128)S(1)}, u32[]{:S(2)}, u32[]{:S(2)}) collective-permute-start(f32[224,128]{1,0:T(8,128)S(1)} %get-tuple-element.31), channel_id=1, source_target_pairs={{0,8},{1,9},{2,10},{3,11},{16,24},{17,25},{18,26},{19,27},{8,0},{9... | collective-permute-start | bytes 344072 | tf_op jit(solution)/shard_map/ppermute | solution.py:35
  39.6 1.0 collective-permute-done.5.refs_3_
  40.5 3.5 %collective-permute-done.6.refs_4_ = f32[224,128]{1,0:T(8,128)S(1)} collective-permute-done((f32[224,128]{1,0:T(8,128)S(1)}, f32[224,128]{1,0:T(8,128)S(1)}, u32[]{:S(2)}, u32[]{:S(2)}) %collective-permute-start.6) | collective-permute-done | bytes 114720 | tf_op jit(solution)/shard_map/ppermute | solution.py:35
  44.1 0.8 round1.1
  44.9 4.1 %collective-permute-start.7 = (f32[192,128]{1,0:T(8,128)S(1)}, f32[192,128]{1,0:T(8,128)S(1)}, u32[]{:S(2)}, u32[]{:S(2)}) collective-permute-start(f32[192,128]{1,0:T(8,128)S(1)} %get-tuple-element.34), channel_id=1, source_target_pairs={{0,8},{1,9},{2,10},{3,11},{16,24},{17,25},{18,26},{19,27},{8,0},{9... | collective-permute-start | bytes 294920 | tf_op jit(solution)/shard_map/ppermute | solution.py:35
  49.0 0.9 collective-permute-done.7.refs_3_
  49.9 3.4 %collective-permute-done.8.refs_4_ = f32[192,128]{1,0:T(8,128)S(1)} collective-permute-done((f32[192,128]{1,0:T(8,128)S(1)}, f32[192,128]{1,0:T(8,128)S(1)}, u32[]{:S(2)}, u32[]{:S(2)}) %collective-permute-start.8) | collective-permute-done | bytes 98336 | tf_op jit(solution)/shard_map/ppermute | solution.py:35
  53.3 0.9 round2.1
  54.2 1.1 %collective-permute-start.9 = (f32[160,128]{1,0:T(8,128)S(1)}, f32[160,128]{1,0:T(8,128)S(1)}, u32[]{:S(2)}, u32[]{:S(2)}) collective-permute-start(f32[160,128]{1,0:T(8,128)S(1)} %get-tuple-element.37), channel_id=1, source_target_pairs={{0,8},{1,9},{2,10},{3,11},{16,24},{17,25},{18,26},{19,27},{8,0},{9... | collective-permute-start | bytes 245768 | tf_op jit(solution)/shard_map/ppermute | solution.py:35
  55.3 1.8 %collective-permute-start.10 = (f32[160,128]{1,0:T(8,128)S(1)}, f32[160,128]{1,0:T(8,128)S(1)}, u32[]{:S(2)}, u32[]{:S(2)}) collective-permute-start(f32[160,128]{1,0:T(8,128)S(1)} %get-tuple-element.38), channel_id=1, source_target_pairs={{0,104},{1,105},{2,106},{3,107},{16,120},{17,121},{18,122},{19,123... | collective-permute-start | bytes 245768 | tf_op jit(solution)/shard_map/ppermute | solution.py:35
  57.1 2.4 %collective-permute-done.10.refs_4_ = f32[160,128]{1,0:T(8,128)S(1)} collective-permute-done((f32[160,128]{1,0:T(8,128)S(1)}, f32[160,128]{1,0:T(8,128)S(1)}, u32[]{:S(2)}, u32[]{:S(2)}) %collective-permute-start.10) | collective-permute-done | bytes 81952 | tf_op jit(solution)/shard_map/ppermute | solution.py:35
  59.5 3.4 %round3.1 = (f32[2,400,128]{2,1,0:T(8,128)S(1)}, f32[128,128]{1,0:T(8,128)S(1)}, f32[128,128]{1,0:T(8,128)S(1)}) custom-call(f32[5,400,128]{2,1,0:T(8,128)S(1)} %get-tuple-element.28.refs_0_.stat, f32[2,400,128]{2,1,0:T(8,128)S(1)} %get-tuple-element.36.refs_1_, f32[24,128]{1,0:T(8,128)S(1)} %get-tuple-element.30.refs_2_.meta, ...), custom_call_target="tpu_custom_call" | custom-call | tf_op jit(solution)/shard_map/round3/pallas_call | solution.py:455
  63.0 1.9 %collective-permute-start.12 = (f32[128,128]{1,0:T(8,128)S(1)}, f32[128,128]{1,0:T(8,128)S(1)}, u32[]{:S(2)}, u32[]{:S(2)}) collective-permute-start(f32[128,128]{1,0:T(8,128)S(1)} %get-tuple-element.41), channel_id=1, source_target_pairs={{0,104},{1,105},{2,106},{3,107},{16,120},{17,121},{18,122},{19,123... | collective-permute-start | bytes 196616 | tf_op jit(solution)/shard_map/ppermute | solution.py:35
  64.8 1.9 %collective-permute-done.12.refs_4_ = f32[128,128]{1,0:T(8,128)S(1)} collective-permute-done((f32[128,128]{1,0:T(8,128)S(1)}, f32[128,128]{1,0:T(8,128)S(1)}, u32[]{:S(2)}, u32[]{:S(2)}) %collective-permute-start.12) | collective-permute-done | bytes 65568 | tf_op jit(solution)/shard_map/ppermute | solution.py:35
  66.8 0.6 round4.1
  67.3 2.4 %collective-permute-start.13 = (f32[96,128]{1,0:T(8,128)S(1)}, f32[96,128]{1,0:T(8,128)S(1)}, u32[]{:S(2)}, u32[]{:S(2)}) collective-permute-start(f32[96,128]{1,0:T(8,128)S(1)} %get-tuple-element.43), channel_id=1, source_target_pairs={{0,8},{1,9},{2,10},{3,11},{16,24},{17,25},{18,26},{19,27},{8,0},{9... | collective-permute-start | bytes 147464 | tf_op jit(solution)/shard_map/ppermute | solution.py:35
  69.7 0.9 collective-permute-done.13.first
  70.6 2.6 %collective-permute-done.14.second = f32[96,128]{1,0:T(8,128)S(1)} collective-permute-done((f32[96,128]{1,0:T(8,128)S(1)}, f32[96,128]{1,0:T(8,128)S(1)}, u32[]{:S(2)}, u32[]{:S(2)}) %collective-permute-start.14) | collective-permute-done | bytes 49184 | tf_op jit(solution)/shard_map/ppermute | solution.py:35
  73.2 0.5 round5.1.nat
  73.7 0.7 collective-permute-start.15
  74.4 0.3 coarse.1
  74.7 23.7 %all_to_all.5.got = f32[128,2,128]{2,1,0:T(2,128)S(1)} all-to-all(f32[128,2,128]{2,1,0:T(2,128)S(1)} %coarse.1), channel_id=1, replica_groups=mesh['gx'=16,'gy'=8] {'gx','gy'}, dimensions={0} | all-to-all | bytes 262144 | tf_op jit(solution)/shard_map/all_to_all | solution.py:470
  98.4 0.9 lift.1
  (16 shorter events, 0.2 us)
Async XLA Ops:
  2.4 16.6 %collective-permute-start = (f32[65,8,128]{2,1,0:T(8,128)S(1)}, f32[65,8,128]{2,1,0:T(8,128)S(1)}, u32[]{:S(2)}, u32[]{:S(2)}) collective-permute-start(f32[65,8,128]{2,1,0:T(8,128)S(1)} %get-tuple-element.24), channel_id=1, source_target_pairs={{0,0},{1,1},{2,2},{3,3},{4,16},{5,17},{6,18},{7,19},{8,8},{9,9},{1... | collective-permute-start | bytes 798728 | tf_op jit(solution)/shard_map/ppermute | solution.py:35
  3.0 12.0 %collective-permute-start.2 = (f32[49,8,128]{2,1,0:T(8,128)S(1)}, f32[49,8,128]{2,1,0:T(8,128)S(1)}, u32[]{:S(2)}, u32[]{:S(2)}) collective-permute-start(f32[49,8,128]{2,1,0:T(8,128)S(1)} %get-tuple-element.25), channel_id=1, source_target_pairs={{0,19},{1,0},{2,1},{3,2},{4,3},{5,16},{6,17},{7,18},{8,27},{9,8},{... | collective-permute-start | bytes 602120 | tf_op jit(solution)/shard_map/ppermute | solution.py:35
  11.6 7.4 %collective-permute-start.1 = (f32[49,8,128]{2,1,0:T(8,128)S(1)}, f32[49,8,128]{2,1,0:T(8,128)S(1)}, u32[]{:S(2)}, u32[]{:S(2)}) collective-permute-start(f32[49,8,128]{2,1,0:T(8,128)S(1)} %get-tuple-element.25), channel_id=1, source_target_pairs={{0,1},{1,2},{2,3},{3,16},{4,17},{5,18},{6,19},{7,0},{8,9},{9,10},{... | collective-permute-start | bytes 602120 | tf_op jit(solution)/shard_map/ppermute | solution.py:35
  19.1 3.8 %collective-permute-start.3 = (f32[27,8,384]{2,1,0:T(8,128)S(1)}, f32[27,8,384]{2,1,0:T(8,128)S(1)}, u32[]{:S(2)}, u32[]{:S(2)}) collective-permute-start(f32[27,8,384]{2,1,0:T(8,128)S(1)} %get-tuple-element.26), channel_id=1, source_target_pairs={{0,8},{1,9},{2,10},{3,11},{16,24},{17,25},{18,26},{19,27},{8,0},{9... | collective-permute-start | bytes 995336 | tf_op jit(solution)/shard_map/ppermute | solution.py:35
  21.3 6.5 %collective-permute-start.4 = (f32[27,8,384]{2,1,0:T(8,128)S(1)}, f32[27,8,384]{2,1,0:T(8,128)S(1)}, u32[]{:S(2)}, u32[]{:S(2)}) collective-permute-start(f32[27,8,384]{2,1,0:T(8,128)S(1)} %get-tuple-element.27), channel_id=1, source_target_pairs={{0,104},{1,105},{2,106},{3,107},{16,120},{17,121},{18,122},{19,123... | collective-permute-start | bytes 995336 | tf_op jit(solution)/shard_map/ppermute | solution.py:35
  31.7 8.8 %collective-permute-start.5 = (f32[224,128]{1,0:T(8,128)S(1)}, f32[224,128]{1,0:T(8,128)S(1)}, u32[]{:S(2)}, u32[]{:S(2)}) collective-permute-start(f32[224,128]{1,0:T(8,128)S(1)} %get-tuple-element.31), channel_id=1, source_target_pairs={{0,8},{1,9},{2,10},{3,11},{16,24},{17,25},{18,26},{19,27},{8,0},{9... | collective-permute-start | bytes 344072 | tf_op jit(solution)/shard_map/ppermute | solution.py:35
  39.6 4.5 %collective-permute-start.6 = (f32[224,128]{1,0:T(8,128)S(1)}, f32[224,128]{1,0:T(8,128)S(1)}, u32[]{:S(2)}, u32[]{:S(2)}) collective-permute-start(f32[224,128]{1,0:T(8,128)S(1)} %get-tuple-element.32), channel_id=1, source_target_pairs={{0,104},{1,105},{2,106},{3,107},{16,120},{17,121},{18,122},{19,123... | collective-permute-start | bytes 344072 | tf_op jit(solution)/shard_map/ppermute | solution.py:35
  44.9 5.0 %collective-permute-start.7 = (f32[192,128]{1,0:T(8,128)S(1)}, f32[192,128]{1,0:T(8,128)S(1)}, u32[]{:S(2)}, u32[]{:S(2)}) collective-permute-start(f32[192,128]{1,0:T(8,128)S(1)} %get-tuple-element.34), channel_id=1, source_target_pairs={{0,8},{1,9},{2,10},{3,11},{16,24},{17,25},{18,26},{19,27},{8,0},{9... | collective-permute-start | bytes 294920 | tf_op jit(solution)/shard_map/ppermute | solution.py:35
  49.0 4.3 %collective-permute-start.8 = (f32[192,128]{1,0:T(8,128)S(1)}, f32[192,128]{1,0:T(8,128)S(1)}, u32[]{:S(2)}, u32[]{:S(2)}) collective-permute-start(f32[192,128]{1,0:T(8,128)S(1)} %get-tuple-element.35), channel_id=1, source_target_pairs={{0,104},{1,105},{2,106},{3,107},{16,120},{17,121},{18,122},{19,123... | collective-permute-start | bytes 294920 | tf_op jit(solution)/shard_map/ppermute | solution.py:35
  54.2 2.9 %collective-permute-start.9 = (f32[160,128]{1,0:T(8,128)S(1)}, f32[160,128]{1,0:T(8,128)S(1)}, u32[]{:S(2)}, u32[]{:S(2)}) collective-permute-start(f32[160,128]{1,0:T(8,128)S(1)} %get-tuple-element.37), channel_id=1, source_target_pairs={{0,8},{1,9},{2,10},{3,11},{16,24},{17,25},{18,26},{19,27},{8,0},{9... | collective-permute-start | bytes 245768 | tf_op jit(solution)/shard_map/ppermute | solution.py:35
  55.3 4.2 %collective-permute-start.10 = (f32[160,128]{1,0:T(8,128)S(1)}, f32[160,128]{1,0:T(8,128)S(1)}, u32[]{:S(2)}, u32[]{:S(2)}) collective-permute-start(f32[160,128]{1,0:T(8,128)S(1)} %get-tuple-element.38), channel_id=1, source_target_pairs={{0,104},{1,105},{2,106},{3,107},{16,120},{17,121},{18,122},{19,123... | collective-permute-start | bytes 245768 | tf_op jit(solution)/shard_map/ppermute | solution.py:35
  62.9 1.9 %collective-permute-start.11 = (f32[128,128]{1,0:T(8,128)S(1)}, f32[128,128]{1,0:T(8,128)S(1)}, u32[]{:S(2)}, u32[]{:S(2)}) collective-permute-start(f32[128,128]{1,0:T(8,128)S(1)} %get-tuple-element.40), channel_id=1, source_target_pairs={{0,8},{1,9},{2,10},{3,11},{16,24},{17,25},{18,26},{19,27},{8,0},{9... | collective-permute-start | bytes 196616 | tf_op jit(solution)/shard_map/ppermute | solution.py:35
  63.0 3.8 %collective-permute-start.12 = (f32[128,128]{1,0:T(8,128)S(1)}, f32[128,128]{1,0:T(8,128)S(1)}, u32[]{:S(2)}, u32[]{:S(2)}) collective-permute-start(f32[128,128]{1,0:T(8,128)S(1)} %get-tuple-element.41), channel_id=1, source_target_pairs={{0,104},{1,105},{2,106},{3,107},{16,120},{17,121},{18,122},{19,123... | collective-permute-start | bytes 196616 | tf_op jit(solution)/shard_map/ppermute | solution.py:35
  67.3 3.2 %collective-permute-start.13 = (f32[96,128]{1,0:T(8,128)S(1)}, f32[96,128]{1,0:T(8,128)S(1)}, u32[]{:S(2)}, u32[]{:S(2)}) collective-permute-start(f32[96,128]{1,0:T(8,128)S(1)} %get-tuple-element.43), channel_id=1, source_target_pairs={{0,8},{1,9},{2,10},{3,11},{16,24},{17,25},{18,26},{19,27},{8,0},{9... | collective-permute-start | bytes 147464 | tf_op jit(solution)/shard_map/ppermute | solution.py:35
  69.7 3.5 %collective-permute-start.14 = (f32[96,128]{1,0:T(8,128)S(1)}, f32[96,128]{1,0:T(8,128)S(1)}, u32[]{:S(2)}, u32[]{:S(2)}) collective-permute-start(f32[96,128]{1,0:T(8,128)S(1)} %get-tuple-element.44), channel_id=1, source_target_pairs={{0,104},{1,105},{2,106},{3,107},{16,120},{17,121},{18,122},{19,123... | collective-permute-start | bytes 147464 | tf_op jit(solution)/shard_map/ppermute | solution.py:35
  73.7 24.7 %collective-permute-start.15 = (f32[4,8,8,128]{3,2,1,0:T(8,128)S(1)}, f32[4,8,8,128]{3,2,1,0:T(8,128)S(1)}, u32[]{:S(2)}, u32[]{:S(2)}) collective-permute-start(f32[4,8,8,128]{3,2,1,0:T(8,128)S(1)} %round5.1.nat), channel_id=1, source_target_pairs={{0,0},{1,1},{2,2},{3,3},{16,4},{17,5},{18,6},{19,7},{8,8},{9,9},{1... | collective-permute-start | bytes 393224 | tf_op jit(solution)/shard_map/ppermute | solution.py:35
  74.7 23.7 %copy-start = (f32[2,8,8,128]{3,2,1,0:T(8,128)S(1)}, f32[2,8,8,128]{3,2,1,0:T(8,128)}, u32[]{:S(2)}) copy-start(f32[2,8,8,128]{3,2,1,0:T(8,128)} %basis.3) | copy-start | bytes 196612
  74.7 23.7 %copy-start.1 = (f32[1,1,2,256]{3,2,1,0:T(2,128)S(1)}, f32[1,1,2,256]{3,2,1,0:T(2,128)}, u32[]{:S(2)}) copy-start(f32[1,1,2,256]{3,2,1,0:T(2,128)} %inv.1) | copy-start | bytes 6148

commit v4 on v2

--- a/solution.py
+++ b/solution.py
@@ -18,16 +18,16 @@
 
 
 def home(i, j):
-    y, a, core = i // 4, i // 2 % 2, i % 2
-    low = a if y % 2 == 0 else 1 - a
+    pair, core = i // 2, i % 2
+    y, low = (pair, 0) if pair < 4 else (7 - pair, 1)
     return (y * 4 + j // 4 * 2 + core) * NGY + low * 4 + j % 4
 
 
 def block_here():
     gx, gy = lax.axis_index("gx"), lax.axis_index("gy")
     y, low = gx // 4, gy // 4
-    a = jnp.where(y % 2 == 0, low, 1 - low)
-    return y * 4 + a * 2 + gx % 2, gx // 2 % 2 * 4 + gy % 4
+    pair = jnp.where(low == 0, y, 7 - y)
+    return pair * 2 + gx % 2, gx // 2 % 2 * 4 + gy % 4
 
 
 def send(x, to):

time: 97.6 us -> 98.6 us (1.010); the launches traced: 99.2 us -> 97.3 us
  waiting for transfers between devices: 37.4 us -> 33.8 us
  starting transfers between devices: 47.8 us -> 49.2 us
    ppermute x16, waiting for transfers between devices: 28.1 us -> 24.5 us  [send(): return lax.ppermute(x, ('gx', 'gy'), [to(i, j) for i, j in blocks])]
    pallas_call x4, Pallas kernels: 5.67 us -> 8.49 us  [shards(): call(lambda *refs, rnd=rnd: middle_kernel(rnd, *refs), (sds(2, ROWS, 128)...]
    pallas_call x1, Pallas kernels: 3.58 us -> 0.85 us  [shards(): call(start_kernel, (sds(5, ROWS, 128), sds(2, ROWS, 128), sds(24, 128), s...]
    ppermute x16, starting transfers between devices: 33.9 us -> 35.5 us  [send(): return lax.ppermute(x, ('gx', 'gy'), [to(i, j) for i, j in blocks])]
  transfers between devices with their start and end apart: 17 -> 17, of which waited for: 12 -> 10; matrix products, arithmetic and copies ran while one was open for 0% -> 0% of each run, Pallas kernels for 0% -> 0%
where the time goes in v4:
time: 98.6 us; the launch traced here: 97.3 us
  starting transfers between devices  49.2 us (50%)
  waiting for transfers between devices  33.8 us (34%)
  Pallas kernels  12.8 us (13%)
  between operations  1.42 us (1%)
    ppermute x16, starting transfers between devices, send(): return lax.ppermute(x, ('gx', 'gy'), [to(i, j) for i, j in blocks])  35.5 us
    ppermute x16, waiting for transfers between devices, send(): return lax.ppermute(x, ('gx', 'gy'), [to(i, j) for i, j in blocks])  24.5 us
    all_to_all x1, starting transfers between devices, shards(): got = lax.all_to_all(rows, ('gx', 'gy'), 0, 0, tiled=True)  13.7 us
    all_to_all x1, waiting for transfers between devices, shards(): got = lax.all_to_all(rows, ('gx', 'gy'), 0, 0, tiled=True)  9.32 us
    pallas_call x4, Pallas kernels, shards(): call(lambda *refs, rnd=rnd: middle_kernel(rnd, *refs), (sds(2, ROWS, 128)...  8.49 us
  transfers between devices with their start and end apart: 17, of which 10 were waited for; matrix products, arithmetic and copies ran while one was open for 0% of the time, Pallas kernels for 0%

profile of v4, /device:TPU:1, one launch (start us, length us, event | category | flops | bytes accessed | tf_op | source)
XLA Modules:
  0.0 97.3 jit_solution(18157458973236085059)
XLA Ops:
  1.3 1.1 %pack.1 = (f32[49,8,128]{2,1,0:T(8,128)S(1)}, f32[65,8,128]{2,1,0:T(8,128)S(1)}) custom-call(f32[3,8,8,128]{3,2,1,0:T(8,128)} %mix.1, f32[2,8,8,128]{3,2,1,0:T(8,128)} %forc.1, s32[8,8,128]{2,1,0:T(8,128)} %lab.1, f32[2,8,8,128]{3,2,1,0:T(8,128)} %basis.3, s32[8,128]{1,0:T(8,128)S(1)} %broadcast_in_dim.8.colour), custom_call_target="tpu_custom_call" | custom-call | tf_op jit(solution)/shard_map/pack/pallas_call | solution.py:425
  2.4 0.7 collective-permute-start
  3.0 9.6 %collective-permute-start.2 = (f32[49,8,128]{2,1,0:T(8,128)S(1)}, f32[49,8,128]{2,1,0:T(8,128)S(1)}, u32[]{:S(2)}, u32[]{:S(2)}) collective-permute-start(f32[49,8,128]{2,1,0:T(8,128)S(1)} %get-tuple-element.25), channel_id=1, source_target_pairs={{0,19},{1,0},{2,1},{3,2},{4,3},{5,16},{6,17},{7,18},{8,27},{9,8},{... | collective-permute-start | bytes 602120 | tf_op jit(solution)/shard_map/ppermute | solution.py:35
  12.6 3.4 %collective-permute-done.2.right = f32[49,8,128]{2,1,0:T(8,128)S(1)} collective-permute-done((f32[49,8,128]{2,1,0:T(8,128)S(1)}, f32[49,8,128]{2,1,0:T(8,128)S(1)}, u32[]{:S(2)}, u32[]{:S(2)}) %collective-permute-start.2) | collective-permute-done | bytes 200736 | tf_op jit(solution)/shard_map/ppermute | solution.py:35
  16.0 3.9 %collective-permute-done.1.left = f32[49,8,128]{2,1,0:T(8,128)S(1)} collective-permute-done((f32[49,8,128]{2,1,0:T(8,128)S(1)}, f32[49,8,128]{2,1,0:T(8,128)S(1)}, u32[]{:S(2)}, u32[]{:S(2)}) %collective-permute-start.1) | collective-permute-done | bytes 200736 | tf_op jit(solution)/shard_map/ppermute | solution.py:35
  20.1 2.2 %collective-permute-start.3 = (f32[27,8,384]{2,1,0:T(8,128)S(1)}, f32[27,8,384]{2,1,0:T(8,128)S(1)}, u32[]{:S(2)}, u32[]{:S(2)}) collective-permute-start(f32[27,8,384]{2,1,0:T(8,128)S(1)} %get-tuple-element.26), channel_id=1, source_target_pairs={{0,8},{1,9},{2,10},{3,11},{16,24},{17,25},{18,26},{19,27},{8,0},{9... | collective-permute-start | bytes 995336 | tf_op jit(solution)/shard_map/ppermute | solution.py:35
  22.3 7.5 %collective-permute-start.4 = (f32[27,8,384]{2,1,0:T(8,128)S(1)}, f32[27,8,384]{2,1,0:T(8,128)S(1)}, u32[]{:S(2)}, u32[]{:S(2)}) collective-permute-start(f32[27,8,384]{2,1,0:T(8,128)S(1)} %get-tuple-element.27), channel_id=1, source_target_pairs={{0,12},{1,13},{2,14},{3,15},{16,28},{17,29},{18,30},{19,31},{8,32}... | collective-permute-start | bytes 995336 | tf_op jit(solution)/shard_map/ppermute | solution.py:35
  29.8 4.8 %collective-permute-done.4.second = f32[27,8,384]{2,1,0:T(8,128)S(1)} collective-permute-done((f32[27,8,384]{2,1,0:T(8,128)S(1)}, f32[27,8,384]{2,1,0:T(8,128)S(1)}, u32[]{:S(2)}, u32[]{:S(2)}) %collective-permute-start.4) | collective-permute-done | bytes 331808 | tf_op jit(solution)/shard_map/ppermute | solution.py:35
  34.6 0.9 round0.1
  35.5 0.4 collective-permute-start.5
  35.9 4.6 %collective-permute-start.6 = (f32[224,128]{1,0:T(8,128)S(1)}, f32[224,128]{1,0:T(8,128)S(1)}, u32[]{:S(2)}, u32[]{:S(2)}) collective-permute-start(f32[224,128]{1,0:T(8,128)S(1)} %get-tuple-element.32), channel_id=1, source_target_pairs={{0,12},{1,13},{2,14},{3,15},{16,28},{17,29},{18,30},{19,31},{8,32}... | collective-permute-start | bytes 344072 | tf_op jit(solution)/shard_map/ppermute | solution.py:35
  40.4 2.5 %collective-permute-done.6.refs_4_ = f32[224,128]{1,0:T(8,128)S(1)} collective-permute-done((f32[224,128]{1,0:T(8,128)S(1)}, f32[224,128]{1,0:T(8,128)S(1)}, u32[]{:S(2)}, u32[]{:S(2)}) %collective-permute-start.6) | collective-permute-done | bytes 114720 | tf_op jit(solution)/shard_map/ppermute | solution.py:35
  42.9 1.0 round1.1
  43.9 0.1 collective-permute-start.7
  44.0 4.5 %collective-permute-start.8 = (f32[192,128]{1,0:T(8,128)S(1)}, f32[192,128]{1,0:T(8,128)S(1)}, u32[]{:S(2)}, u32[]{:S(2)}) collective-permute-start(f32[192,128]{1,0:T(8,128)S(1)} %get-tuple-element.35), channel_id=1, source_target_pairs={{0,12},{1,13},{2,14},{3,15},{16,28},{17,29},{18,30},{19,31},{8,32}... | collective-permute-start | bytes 294920 | tf_op jit(solution)/shard_map/ppermute | solution.py:35
  48.5 2.3 %collective-permute-done.8.refs_4_ = f32[192,128]{1,0:T(8,128)S(1)} collective-permute-done((f32[192,128]{1,0:T(8,128)S(1)}, f32[192,128]{1,0:T(8,128)S(1)}, u32[]{:S(2)}, u32[]{:S(2)}) %collective-permute-start.8) | collective-permute-done | bytes 98336 | tf_op jit(solution)/shard_map/ppermute | solution.py:35
  50.8 6.1 %round2.1 = (f32[2,400,128]{2,1,0:T(8,128)S(1)}, f32[160,128]{1,0:T(8,128)S(1)}, f32[160,128]{1,0:T(8,128)S(1)}) custom-call(f32[5,400,128]{2,1,0:T(8,128)S(1)} %get-tuple-element.28.refs_0_.stat, f32[2,400,128]{2,1,0:T(8,128)S(1)} %get-tuple-element.33.refs_1_, f32[24,128]{1,0:T(8,128)S(1)} %get-tuple-element.30.refs_2_.meta, ...), custom_call_target="tpu_custom_call" | custom-call | tf_op jit(solution)/shard_map/round2/pallas_call | solution.py:453
  57.1 1.2 %collective-permute-done.9.refs_3_ = f32[160,128]{1,0:T(8,128)S(1)} collective-permute-done((f32[160,128]{1,0:T(8,128)S(1)}, f32[160,128]{1,0:T(8,128)S(1)}, u32[]{:S(2)}, u32[]{:S(2)}) %collective-permute-start.9) | collective-permute-done | bytes 81952 | tf_op jit(solution)/shard_map/ppermute | solution.py:35
  58.3 2.7 %collective-permute-done.10.refs_4_ = f32[160,128]{1,0:T(8,128)S(1)} collective-permute-done((f32[160,128]{1,0:T(8,128)S(1)}, f32[160,128]{1,0:T(8,128)S(1)}, u32[]{:S(2)}, u32[]{:S(2)}) %collective-permute-start.10) | collective-permute-done | bytes 81952 | tf_op jit(solution)/shard_map/ppermute | solution.py:35
  61.0 0.9 round3.1
  61.8 0.5 collective-permute-start.11
  62.3 2.4 %collective-permute-start.12 = (f32[128,128]{1,0:T(8,128)S(1)}, f32[128,128]{1,0:T(8,128)S(1)}, u32[]{:S(2)}, u32[]{:S(2)}) collective-permute-start(f32[128,128]{1,0:T(8,128)S(1)} %get-tuple-element.41), channel_id=1, source_target_pairs={{0,12},{1,13},{2,14},{3,15},{16,28},{17,29},{18,30},{19,31},{8,32}... | collective-permute-start | bytes 196616 | tf_op jit(solution)/shard_map/ppermute | solution.py:35
  64.7 1.9 %collective-permute-done.12.refs_4_ = f32[128,128]{1,0:T(8,128)S(1)} collective-permute-done((f32[128,128]{1,0:T(8,128)S(1)}, f32[128,128]{1,0:T(8,128)S(1)}, u32[]{:S(2)}, u32[]{:S(2)}) %collective-permute-start.12) | collective-permute-done | bytes 65568 | tf_op jit(solution)/shard_map/ppermute | solution.py:35
  66.7 0.6 round4.1
  67.3 2.1 %collective-permute-start.14 = (f32[96,128]{1,0:T(8,128)S(1)}, f32[96,128]{1,0:T(8,128)S(1)}, u32[]{:S(2)}, u32[]{:S(2)}) collective-permute-start(f32[96,128]{1,0:T(8,128)S(1)} %get-tuple-element.44), channel_id=1, source_target_pairs={{0,12},{1,13},{2,14},{3,15},{16,28},{17,29},{18,30},{19,31},{8,32}... | collective-permute-start | bytes 147464 | tf_op jit(solution)/shard_map/ppermute | solution.py:35
  69.5 1.8 %collective-permute-done.14.second = f32[96,128]{1,0:T(8,128)S(1)} collective-permute-done((f32[96,128]{1,0:T(8,128)S(1)}, f32[96,128]{1,0:T(8,128)S(1)}, u32[]{:S(2)}, u32[]{:S(2)}) %collective-permute-start.14) | collective-permute-done | bytes 49184 | tf_op jit(solution)/shard_map/ppermute | solution.py:35
  71.2 0.5 round5.1.nat
  71.7 0.9 coarse.1
  72.7 13.7 %all-to-all-start = ((f32[128,2,128]{2,1,0:T(2,128)}), f32[128,2,128]{2,1,0:T(2,128)S(1)}, u32[]{:S(2)}, u32[]{:S(2)}) async-start(f32[128,2,128]{2,1,0:T(2,128)} %coarse.1), calls=%async_computation | async-start | bytes 262144 | tf_op jit(solution)/shard_map/all_to_all | solution.py:468
  86.4 0.7 collective-permute-start.15
  87.0 9.3 %all-to-all-done.got = f32[128,2,128]{2,1,0:T(2,128)S(1)} async-done(((f32[128,2,128]{2,1,0:T(2,128)}), f32[128,2,128]{2,1,0:T(2,128)S(1)}, u32[]{:S(2)}, u32[]{:S(2)}) %all-to-all-start) | async-done | bytes 131104 | tf_op jit(solution)/shard_map/all_to_all | solution.py:468
  96.4 0.9 lift.1
  (17 shorter events, 0.4 us)
Async XLA Ops:
  2.4 17.6 %collective-permute-start = (f32[65,8,128]{2,1,0:T(8,128)S(1)}, f32[65,8,128]{2,1,0:T(8,128)S(1)}, u32[]{:S(2)}, u32[]{:S(2)}) collective-permute-start(f32[65,8,128]{2,1,0:T(8,128)S(1)} %get-tuple-element.24), channel_id=1, source_target_pairs={{0,0},{1,1},{2,2},{3,3},{4,16},{5,17},{6,18},{7,19},{8,8},{9,9},{1... | collective-permute-start | bytes 798728 | tf_op jit(solution)/shard_map/ppermute | solution.py:35
  3.0 13.0 %collective-permute-start.2 = (f32[49,8,128]{2,1,0:T(8,128)S(1)}, f32[49,8,128]{2,1,0:T(8,128)S(1)}, u32[]{:S(2)}, u32[]{:S(2)}) collective-permute-start(f32[49,8,128]{2,1,0:T(8,128)S(1)} %get-tuple-element.25), channel_id=1, source_target_pairs={{0,19},{1,0},{2,1},{3,2},{4,3},{5,16},{6,17},{7,18},{8,27},{9,8},{... | collective-permute-start | bytes 602120 | tf_op jit(solution)/shard_map/ppermute | solution.py:35
  12.6 7.4 %collective-permute-start.1 = (f32[49,8,128]{2,1,0:T(8,128)S(1)}, f32[49,8,128]{2,1,0:T(8,128)S(1)}, u32[]{:S(2)}, u32[]{:S(2)}) collective-permute-start(f32[49,8,128]{2,1,0:T(8,128)S(1)} %get-tuple-element.25), channel_id=1, source_target_pairs={{0,1},{1,2},{2,3},{3,16},{4,17},{5,18},{6,19},{7,0},{8,9},{9,10},{... | collective-permute-start | bytes 602120 | tf_op jit(solution)/shard_map/ppermute | solution.py:35
  20.1 9.7 %collective-permute-start.3 = (f32[27,8,384]{2,1,0:T(8,128)S(1)}, f32[27,8,384]{2,1,0:T(8,128)S(1)}, u32[]{:S(2)}, u32[]{:S(2)}) collective-permute-start(f32[27,8,384]{2,1,0:T(8,128)S(1)} %get-tuple-element.26), channel_id=1, source_target_pairs={{0,8},{1,9},{2,10},{3,11},{16,24},{17,25},{18,26},{19,27},{8,0},{9... | collective-permute-start | bytes 995336 | tf_op jit(solution)/shard_map/ppermute | solution.py:35
  22.3 12.3 %collective-permute-start.4 = (f32[27,8,384]{2,1,0:T(8,128)S(1)}, f32[27,8,384]{2,1,0:T(8,128)S(1)}, u32[]{:S(2)}, u32[]{:S(2)}) collective-permute-start(f32[27,8,384]{2,1,0:T(8,128)S(1)} %get-tuple-element.27), channel_id=1, source_target_pairs={{0,12},{1,13},{2,14},{3,15},{16,28},{17,29},{18,30},{19,31},{8,32}... | collective-permute-start | bytes 995336 | tf_op jit(solution)/shard_map/ppermute | solution.py:35
  35.5 5.0 %collective-permute-start.5 = (f32[224,128]{1,0:T(8,128)S(1)}, f32[224,128]{1,0:T(8,128)S(1)}, u32[]{:S(2)}, u32[]{:S(2)}) collective-permute-start(f32[224,128]{1,0:T(8,128)S(1)} %get-tuple-element.31), channel_id=1, source_target_pairs={{0,8},{1,9},{2,10},{3,11},{16,24},{17,25},{18,26},{19,27},{8,0},{9... | collective-permute-start | bytes 344072 | tf_op jit(solution)/shard_map/ppermute | solution.py:35
  35.9 7.0 %collective-permute-start.6 = (f32[224,128]{1,0:T(8,128)S(1)}, f32[224,128]{1,0:T(8,128)S(1)}, u32[]{:S(2)}, u32[]{:S(2)}) collective-permute-start(f32[224,128]{1,0:T(8,128)S(1)} %get-tuple-element.32), channel_id=1, source_target_pairs={{0,12},{1,13},{2,14},{3,15},{16,28},{17,29},{18,30},{19,31},{8,32}... | collective-permute-start | bytes 344072 | tf_op jit(solution)/shard_map/ppermute | solution.py:35
  43.9 4.6 %collective-permute-start.7 = (f32[192,128]{1,0:T(8,128)S(1)}, f32[192,128]{1,0:T(8,128)S(1)}, u32[]{:S(2)}, u32[]{:S(2)}) collective-permute-start(f32[192,128]{1,0:T(8,128)S(1)} %get-tuple-element.34), channel_id=1, source_target_pairs={{0,8},{1,9},{2,10},{3,11},{16,24},{17,25},{18,26},{19,27},{8,0},{9... | collective-permute-start | bytes 294920 | tf_op jit(solution)/shard_map/ppermute | solution.py:35
  44.0 6.8 %collective-permute-start.8 = (f32[192,128]{1,0:T(8,128)S(1)}, f32[192,128]{1,0:T(8,128)S(1)}, u32[]{:S(2)}, u32[]{:S(2)}) collective-permute-start(f32[192,128]{1,0:T(8,128)S(1)} %get-tuple-element.35), channel_id=1, source_target_pairs={{0,12},{1,13},{2,14},{3,15},{16,28},{17,29},{18,30},{19,31},{8,32}... | collective-permute-start | bytes 294920 | tf_op jit(solution)/shard_map/ppermute | solution.py:35
  56.9 1.4 %collective-permute-start.9 = (f32[160,128]{1,0:T(8,128)S(1)}, f32[160,128]{1,0:T(8,128)S(1)}, u32[]{:S(2)}, u32[]{:S(2)}) collective-permute-start(f32[160,128]{1,0:T(8,128)S(1)} %get-tuple-element.37), channel_id=1, source_target_pairs={{0,8},{1,9},{2,10},{3,11},{16,24},{17,25},{18,26},{19,27},{8,0},{9... | collective-permute-start | bytes 245768 | tf_op jit(solution)/shard_map/ppermute | solution.py:35
  57.0 4.0 %collective-permute-start.10 = (f32[160,128]{1,0:T(8,128)S(1)}, f32[160,128]{1,0:T(8,128)S(1)}, u32[]{:S(2)}, u32[]{:S(2)}) collective-permute-start(f32[160,128]{1,0:T(8,128)S(1)} %get-tuple-element.38), channel_id=1, source_target_pairs={{0,12},{1,13},{2,14},{3,15},{16,28},{17,29},{18,30},{19,31},{8,32}... | collective-permute-start | bytes 245768 | tf_op jit(solution)/shard_map/ppermute | solution.py:35
  61.8 2.9 %collective-permute-start.11 = (f32[128,128]{1,0:T(8,128)S(1)}, f32[128,128]{1,0:T(8,128)S(1)}, u32[]{:S(2)}, u32[]{:S(2)}) collective-permute-start(f32[128,128]{1,0:T(8,128)S(1)} %get-tuple-element.40), channel_id=1, source_target_pairs={{0,8},{1,9},{2,10},{3,11},{16,24},{17,25},{18,26},{19,27},{8,0},{9... | collective-permute-start | bytes 196616 | tf_op jit(solution)/shard_map/ppermute | solution.py:35
  62.3 4.4 %collective-permute-start.12 = (f32[128,128]{1,0:T(8,128)S(1)}, f32[128,128]{1,0:T(8,128)S(1)}, u32[]{:S(2)}, u32[]{:S(2)}) collective-permute-start(f32[128,128]{1,0:T(8,128)S(1)} %get-tuple-element.41), channel_id=1, source_target_pairs={{0,12},{1,13},{2,14},{3,15},{16,28},{17,29},{18,30},{19,31},{8,32}... | collective-permute-start | bytes 196616 | tf_op jit(solution)/shard_map/ppermute | solution.py:35
  67.2 2.2 %collective-permute-start.13 = (f32[96,128]{1,0:T(8,128)S(1)}, f32[96,128]{1,0:T(8,128)S(1)}, u32[]{:S(2)}, u32[]{:S(2)}) collective-permute-start(f32[96,128]{1,0:T(8,128)S(1)} %get-tuple-element.43), channel_id=1, source_target_pairs={{0,8},{1,9},{2,10},{3,11},{16,24},{17,25},{18,26},{19,27},{8,0},{9... | collective-permute-start | bytes 147464 | tf_op jit(solution)/shard_map/ppermute | solution.py:35
  67.3 3.9 %collective-permute-start.14 = (f32[96,128]{1,0:T(8,128)S(1)}, f32[96,128]{1,0:T(8,128)S(1)}, u32[]{:S(2)}, u32[]{:S(2)}) collective-permute-start(f32[96,128]{1,0:T(8,128)S(1)} %get-tuple-element.44), channel_id=1, source_target_pairs={{0,12},{1,13},{2,14},{3,15},{16,28},{17,29},{18,30},{19,31},{8,32}... | collective-permute-start | bytes 147464 | tf_op jit(solution)/shard_map/ppermute | solution.py:35
  72.7 23.7 %copy-start = (f32[2,8,8,128]{3,2,1,0:T(8,128)S(1)}, f32[2,8,8,128]{3,2,1,0:T(8,128)}, u32[]{:S(2)}) copy-start(f32[2,8,8,128]{3,2,1,0:T(8,128)} %basis.3) | copy-start | bytes 196612
  72.7 23.7 %copy-start.1 = (f32[1,1,2,256]{3,2,1,0:T(2,128)S(1)}, f32[1,1,2,256]{3,2,1,0:T(2,128)}, u32[]{:S(2)}) copy-start(f32[1,1,2,256]{3,2,1,0:T(2,128)} %inv.1) | copy-start | bytes 6148
  72.7 23.7 %all-to-all-start = ((f32[128,2,128]{2,1,0:T(2,128)}), f32[128,2,128]{2,1,0:T(2,128)S(1)}, u32[]{:S(2)}, u32[]{:S(2)}) async-start(f32[128,2,128]{2,1,0:T(2,128)} %coarse.1), calls=%async_computation | async-start | bytes 262144 | tf_op jit(solution)/shard_map/all_to_all | solution.py:468
  86.4 0.7 collective-permute-start.15
